TPU v7x, 256 devices: a whole 4x4x8 slice. The times are simulated.
256 devices in a mesh: tm: 32 (over x, y, core), space: 8 (over z).
Axes of the slice: x: 4, y: 4, z: 8, core: 2. Of those that a mesh axis runs over, the one named last changes fastest.
Arguments:
- queries: bfloat16 [32, 64, 80, 2240], P('tm', 'space'), may hold values from -6 to 6
- keys: bfloat16 [32, 64, 80, 2240], P('tm', 'space'), may hold values from -60 to 60
- values: bfloat16 [32, 64, 80, 2240], P('tm', 'space'), may hold values from -6 to 6
- conv_weight: float32 [3, 3, 2240], replicated, may hold values from -5 to 5
- w_out: bfloat16 [2240, 2240], P('tm', 'space'), may hold values from -0.125 to 0.125
Outputs:
- layer_out: bfloat16 [32, 64, 80, 2240], P('tm', 'space')
All inputs are finite; a program needn't handle non-finite values.
Results may differ from a plain program's by a relative error of at most 0.001.
The roundings to bfloat16 on the way count: a program that leaves them out, or rounds other values in their place, can miss the bound.
Values may be sent and summed in bfloat16 or wider, within the bound.
A program may use at most 128 MiB of HBM per device.

v0:
```python
import math

import jax
import jax.numpy as jnp
from jax import lax
from jax.sharding import Mesh
from jax.sharding import PartitionSpec as P

HEADS = 20
TM = ("tm_0", "tm_1", "tm_2")


epsilon = 1e-06


def split_up(x, dim, length):
    lengths = x.shape
    parts = x.reshape(*lengths[:dim], length, lengths[dim] // length, *lengths[dim + 1 :])
    return jnp.moveaxis(parts, dim, 0)


def summed_on_arrival(x, axis, dim):
    parts = split_up(x, dim, lax.axis_size(axis))
    arrived = lax.all_to_all(parts, axis, split_axis=0, concat_axis=0, tiled=True)
    return arrived.sum(axis=0)


def side_by_side(arrays, axis, dim, along):
    columns = [a.reshape(*a.shape[:along], -1) for a in arrays]
    both = jnp.concatenate(columns, axis=along)
    result, at, done = (summed_on_arrival(both, axis, dim), 0, [])
    for a, column in zip(arrays, columns):
        share = result[..., at : at + column.shape[along]]
        done.append(share.reshape(*share.shape[:along], *a.shape[along:]))
        at += column.shape[along]
    return tuple(done)


def nothing_yet(x, identity):
    return jax.tree.map(
        lambda a, e: jnp.broadcast_to(jnp.asarray(e, a.dtype), a.shape), x, identity
    )


def entering(x, axes, combine, identity):
    before = start = nothing_yet(x, identity)
    total = x
    for axis in reversed(axes):
        length, position = (lax.axis_size(axis), lax.axis_index(axis))
        pieces = jax.tree.map(lambda part: lax.all_gather(part, axis), total)
        inside, total = (start, start)
        for k in range(length):
            passed = k < position
            total = combine(total, jax.tree.map(lambda part: part[k], pieces))
            inside = jax.tree.map(lambda new, old: jnp.where(passed, new, old), total, inside)
        before = combine(inside, before)
    return before


def side_by_side_2(arrays, axis, dim, along):
    widths = [math.prod(a.shape[along:]) for a in arrays]
    both = jnp.concatenate(
        [a.reshape(*a.shape[:along], w) for a, w in zip(arrays, widths)], axis=along
    )
    result = lax.all_gather(both, axis, axis=dim, tiled=True)
    parts = jnp.split(result, [sum(widths[:k]) for k in range(1, len(widths))], axis=along)
    return tuple(
        (b.reshape(*result.shape[:along], *a.shape[along:]) for a, b in zip(arrays, parts))
    )


def with_halo(cells, sides, width):
    for axis, dim in sides:
        count = lax.axis_size(axis)
        ends = count - 1
        head = lax.slice_in_dim(cells, 0, width, axis=dim)
        tail = lax.slice_in_dim(cells, cells.shape[dim] - width, cells.shape[dim], axis=dim)
        cells = jnp.concatenate(
            [
                lax.ppermute(tail, axis, [(i, (i + 1) % count) for i in range(ends)]),
                cells,
                lax.ppermute(head, axis, [((i + 1) % count, i) for i in range(ends)]),
            ],
            axis=dim,
        )
    return cells


def laid_out(parts, dim):
    lengths = list(parts.shape[1:])
    lengths[dim] *= parts.shape[0]
    return jnp.moveaxis(parts, 0, dim).reshape(lengths)


def sent_to_all(x, axis):
    length = lax.axis_size(axis)
    return lax.all_to_all(jnp.broadcast_to(x[None], (length, *x.shape)), axis, 0, 0, tiled=True)


def gathered_copies(x, axis, dim):
    return laid_out(sent_to_all(x, axis), dim)


def combine_pair(earlier, later):
    return (earlier[0] + later[0], earlier[1] + later[1])


def shards(queries, keys, values, conv_weight, w_out):
    frame_count, row_count, col_count, feature_count = queries.shape
    head_count = HEADS
    head_size = feature_count // head_count
    token_count = row_count * col_count
    key_pos = jnp.maximum(keys, 0).reshape(token_count, head_count, head_size)
    value_heads = values.reshape(token_count, head_count, head_size)
    local_state = jnp.einsum(
        "the,thf->hef", key_pos, value_heads, preferred_element_type=jnp.float32
    )
    local_sum = jnp.sum(key_pos, axis=0, dtype=jnp.float32)
    share_state, share_keys = side_by_side((local_state, local_sum), "space", 1, 2)
    empty = (jnp.zeros_like(share_state), jnp.zeros_like(share_keys))
    before_state, before_keys = entering((share_state, share_keys), TM, combine_pair, empty)
    slice_state = (before_state + share_state).astype(jnp.bfloat16)
    slice_keys = (before_keys + share_keys).astype(jnp.bfloat16)
    state_low, keys_low = side_by_side_2((slice_state, slice_keys), "space", 1, 2)
    query_pos = jnp.maximum(queries, 0).reshape(token_count, head_count, head_size)
    numer = jnp.einsum("the,hef->thf", query_pos, state_low, preferred_element_type=jnp.float32)
    denom = jnp.einsum("the,he->th", query_pos, keys_low, preferred_element_type=jnp.float32)
    attn = (numer / (denom[:, :, None] + epsilon)).reshape(row_count, col_count, feature_count)
    with_rims = with_halo(values[0], (("space", 0),), 1)
    padded = jnp.pad(with_rims, ((0, 0), (1, 1), (0, 0)))
    conv = jnp.zeros((row_count, col_count, feature_count), jnp.float32)
    for row_off in range(3):
        for col_off in range(3):
            window = padded[row_off : row_off + row_count, col_off : col_off + col_count].astype(
                jnp.float32
            )
            conv = conv + window * conv_weight[row_off, col_off]
    mix = (attn + conv).astype(jnp.bfloat16).reshape(token_count, feature_count)
    weight_block = gathered_copies(w_out, "space", 1)
    result = jnp.dot(
        mix,
        lax.all_gather(weight_block, TM, axis=0, tiled=True),
        preferred_element_type=jnp.float32,
    )
    return result.astype(jnp.bfloat16).reshape(1, row_count, col_count, feature_count)


def solution(mesh):
    split = Mesh(
        mesh.devices.reshape(4, 4, 2, mesh.shape["space"]), ("tm_0", "tm_1", "tm_2", "space")
    )
    placed = (
        P(TM, "space", None, None),
        P(TM, "space", None, None),
        P(TM, "space", None, None),
        P(),
        P(TM, "space"),
    )
    return jax.shard_map(
        shards, mesh=split, in_specs=placed, out_specs=P(TM, "space", None, None), check_vma=False
    )
```

profile of v0, /device:TPU:32, one launch (start us, length us, event | category | flops | bytes accessed | tf_op | source)
XLA Modules:
  0.0 280.3 jit_solution(7568035523529269387)
XLA Ops:
  6.5 0.0 all-gather.7.cloned.1.call-start
  6.5 1.0 broadcast_in_dim.15
  7.5 22.6 %all_to_all.10 = bf16[8,70,280]{2,1,0:T(8,128)(2,1)S(1)} all-to-all(bf16[8,70,280]{2,1,0:T(8,128)(2,1)S(1)} %broadcast_in_dim.15), channel_id=1, replica_groups=mesh['tm_0'=4,'tm_1'=4,'tm_2'=2,'space'=8] {'space'}, dimensions={0} | all-to-all | bytes 627200 | tf_op jit(solution)/shard_map/all_to_all | solution.py:97
  30.2 0.1 copy.60
  30.2 1.2 reshape.291
  31.4 0.0 all-gather.7.cloned.1.call-update
  31.4 0.0 copy-done.1
  31.4 1.8 broadcast_maximum_fusion.1
  33.2 7.7 %reshape.243 = bf16[640,20,112]{2,1,0:T(8,128)(2,1)} reshape(bf16[1,8,80,2240]{3,2,1,0:T(8,128)(2,1)} %broadcast_maximum_fusion.1) | data formatting | bytes 5734400 | tf_op jit(solution)/shard_map/reshape | solution.py:113
  41.0 0.0 copy-done
  41.0 5.1 %reshape.244 = bf16[640,20,112]{2,1,0:T(8,128)(2,1)} reshape(bf16[1,8,80,2240]{3,2,1,0:T(8,128)(2,1)S(1)} %copy-done) | data formatting | bytes 5734400 | tf_op jit(solution)/shard_map/reshape | solution.py:114
  46.1 6.1 %fusion.6 = f32[20,112,112]{2,1,0:T(8,128)} fusion(bf16[640,20,112]{2,1,0:T(8,128)(2,1)} %reshape.244, bf16[640,20,112]{2,1,0:T(8,128)(2,1)} %reshape.243), kind=kOutput, calls=%fused_computation.12 | convolution fusion | flops 321126400 | bytes 6737920 | tf_op jit(solution)/shard_map/the,thf->hef/dot_general | solution.py:115
  52.2 2.4 concatenate.20
  54.6 2.5 convert_reduce_fusion
  57.0 1.5 concatenate.27
  58.6 2.1 maximum_bitcast_fusion
  60.7 1.2 copy.45
  61.9 5.5 %all-to-all-start = ((f32[8,20,14,113]{3,2,1,0:T(8,128)}), f32[8,20,14,113]{3,2,1,0:T(8,128)}, u32[]{:S(2)}, u32[]{:S(2)}) async-start(f32[8,20,14,113]{3,2,1,0:T(8,128)} %copy.45), calls=%async_computation | async-start | bytes 2621440 | tf_op jit(solution)/shard_map/all_to_all | solution.py:24
  67.4 0.9 slice_bitcast_fusion.1
  68.3 3.4 %collective-permute-start = (bf16[1,80,2240]{2,1,0:T(8,128)(2,1)}, bf16[1,80,2240]{2,1,0:T(8,128)(2,1)S(1)}, u32[]{:S(2)}, u32[]{:S(2)}) collective-permute-start(bf16[1,80,2240]{2,1,0:T(8,128)(2,1)} %get-tuple-element.14), channel_id=1, source_target_pairs={{0,1},{1,2},{2,3},{3,4},{4,5},{5,6},{6,7},{8,9},{9,10},{10,11},{11... | collective-permute-start | bytes 1075208 | tf_op jit(solution)/shard_map/ppermute | solution.py:80
  71.7 2.5 collective-permute-start.1
  74.2 3.8 %broadcast_maximum_fusion = bf16[1,8,80,2240]{3,2,1,0:T(8,128)(2,1)} fusion(bf16[1,8,80,2240]{3,2,1,0:T(8,128)(2,1)} %param.5), kind=kLoop, calls=%fused_computation.17 | loop fusion | flops 1433600 | bytes 5734400 | tf_op jit(solution)/shard_map/max | solution.py:125
  78.0 7.7 %reshape.245 = bf16[640,20,112]{2,1,0:T(8,128)(2,1)} reshape(bf16[1,8,80,2240]{3,2,1,0:T(8,128)(2,1)} %broadcast_maximum_fusion) | data formatting | bytes 5734400 | tf_op jit(solution)/shard_map/reshape | solution.py:125
  85.6 6.0 %copy.57 = bf16[640,20,112]{0,2,1:T(8,128)(2,1)} copy(bf16[640,20,112]{2,1,0:T(8,128)(2,1)} %reshape.245) | data formatting | bytes 5734400 | tf_op jit(solution)/shard_map/reshape | solution.py:125
  91.7 0.8 slice_reduce_fusion.8
  92.5 10.0 %collective-permute-done = bf16[1,80,2240]{2,1,0:T(8,128)(2,1)S(1)} collective-permute-done((bf16[1,80,2240]{2,1,0:T(8,128)(2,1)}, bf16[1,80,2240]{2,1,0:T(8,128)(2,1)S(1)}, u32[]{:S(2)}, u32[]{:S(2)}) %collective-permute-start) | collective-permute-done | bytes 358432 | tf_op jit(solution)/shard_map/ppermute | solution.py:80
  102.5 1.2 collective-permute-done.1
  103.7 3.9 %fusion.5 = bf16[10,82,2240]{2,1,0:T(8,128)(2,1)} fusion(bf16[1,80,2240]{2,1,0:T(8,128)(2,1)} %collective-permute-done.1, bf16[8,80,2240]{2,1,0:T(8,128)(2,1)S(1)} %bitcast.62, bf16[1,80,2240]{2,1,0:T(8,128)(2,1)S(1)} %collective-permute-done), kind=kLoop, calls=%fused_computation.11 | loop fusion | flops 22041600 | bytes 7257600 | tf_op jit(solution)/shard_map/concatenate | solution.py:78
  107.5 0.0 all-to-all-done
  107.5 1.4 reduce_sum.19
  109.0 0.8 slice.201
  109.8 1.1 copy.47
  110.9 1.8 all-gather.1
  112.7 12.5 %all-gather.3 = f32[80,14,1]{1,2,0:T(1,128)S(1)} all-gather(f32[20,14,1]{1,2,0:T(1,128)S(1)} %slice_add_fusion.10), channel_id=5, replica_groups=mesh['tm_0'=4,'tm_1'=4,'tm_2'=2,'space'=8] {'tm_1'}, dimensions={0}, use_global_device_ids=true | all-gather | bytes 5600 | tf_op jit(solution)/shard_map/all_gather | solution.py:50
  125.2 0.6 fusion.22
  125.8 1.4 copy.48
  127.2 12.4 %all_gather.37 = f32[4,20,14]{1,2,0:T(8,128)S(1)} all-gather(f32[1,20,14]{1,2,0:T(8,128)} %copy.48), channel_id=1, replica_groups=mesh['tm_0'=4,'tm_1'=4,'tm_2'=2,'space'=8] {'tm_0'}, dimensions={0}, use_global_device_ids=true | all-gather | bytes 5600 | tf_op jit(solution)/shard_map/all_gather | solution.py:50
  139.6 0.6 fusion.23
  140.2 1.4 copy.68
  141.6 1.4 copy.69
  143.0 1.4 copy.70
  144.4 1.4 copy.71
  145.7 1.4 fusion.19
  147.1 0.8 copy.53
  147.9 0.9 copy.54
  148.8 2.0 all-gather
  150.9 13.2 %all-gather.2 = f32[80,14,112]{2,1,0:T(8,128)S(1)} all-gather(f32[20,14,112]{2,1,0:T(8,128)S(1)} %slice_add_fusion.6), channel_id=4, replica_groups=mesh['tm_0'=4,'tm_1'=4,'tm_2'=2,'space'=8] {'tm_1'}, dimensions={0}, use_global_device_ids=true | all-gather | bytes 627200 | tf_op jit(solution)/shard_map/all_gather | solution.py:50
  164.1 13.8 %all_gather.34 = f32[4,20,14,112]{3,2,1,0:T(8,128)S(1)} all-gather(f32[1,20,14,112]{3,2,1,0:T(8,128)S(1)} %fusion.17), channel_id=1, replica_groups=mesh['tm_0'=4,'tm_1'=4,'tm_2'=2,'space'=8] {'tm_0'}, dimensions={0}, use_global_device_ids=true | all-gather | bytes 627200 | tf_op jit(solution)/shard_map/all_gather | solution.py:50
  177.9 1.0 add_convert_fusion.1
  179.0 0.1 fusion.16
  179.1 0.1 pad_maximum_fusion.2
  179.2 27.0 %all_gather.38 = bf16[20,112,113]{2,0,1:T(8,128)(2,1)S(1)} all-gather(bf16[20,14,113]{2,0,1:T(8,128)(2,1)S(1)} %copy.55), channel_id=1, replica_groups=mesh['tm_0'=4,'tm_1'=4,'tm_2'=2,'space'=8] {'space'}, dimensions={1}, use_global_device_ids=true | all-gather | bytes 569520 | tf_op jit(solution)/shard_map/all_gather | solution.py:65
  206.2 0.2 split.9
  206.5 0.0 copy-done.2
  206.5 0.6 fusion.9
  207.1 3.4 %bitcast_divide_fusion = f32[640,20,112]{0,2,1:T(8,128)} fusion(f32[640,20]{0,1:T(8,128)S(1)} %fusion.18, bf16[640,20,112]{0,2,1:T(8,128)(2,1)S(1)} %copy-done.2, bf16[20,112,112]{2,0,1:T(8,128)(2,1)S(1)} %bitcast.66), kind=kOutput, calls=%fused_computation.5 | convolution fusion | flops 322560000 | bytes 9154560 | tf_op jit(solution)/shard_map/the,hef->thf/dot_general | solution.py:126
  210.5 9.8 %reshape.308 = f32[8,80,2240]{1,0,2:T(8,128)} reshape(f32[640,20,112]{0,2,1:T(8,128)} %bitcast_divide_fusion) | data formatting | bytes 11468800 | tf_op jit(solution)/shard_map/reshape | solution.py:128
  220.4 8.6 %copy.64 = f32[8,80,2240]{2,1,0:T(8,128)} copy(f32[8,80,2240]{1,0,2:T(8,128)} %reshape.308) | data formatting | bytes 11468800 | tf_op jit(solution)/shard_map/reshape | solution.py:128
  229.0 0.0 copy-done.6
  229.1 14.5 %add_convert_fusion = bf16[8,80,2240]{2,1,0:T(8,128)(2,1)} fusion(f32[8,80,2240]{2,1,0:T(8,128)} %copy.64, bf16[8,80,2240]{2,1,0:T(8,128)(2,1)S(1)} %bitcast.63, bf16[10,82,2240]{2,1,0:T(8,128)(2,1)} %fusion.5, bf16[1,80,2240]{2,1,0:T(8,128)(2,1)} %collective-permute-done.1, bf16[1,80,2240]{2,1,0:T(8,128)(2,1)S(1)} %collective-permute-done, ...), kind=kLoop, calls=%fused_computation.3 | loop fusion | flops 43008000 | bytes 29469440 | tf_op jit(solution)/shard_map/convert_element_type | solution.py:138
  243.5 0.0 all-gather.7.cloned.1.call-done
  243.5 12.2 %reshape.292 = bf16[2240,2240]{1,0:T(8,128)(2,1)} reshape(bf16[32,70,2240]{2,1,0:T(8,128)(2,1)} %all-gather.7.cloned.1.call-done) | data formatting | bytes 20070400
  255.8 12.3 %convolution_convert_fusion = bf16[640,2240]{0,1:T(8,128)(2,1)} fusion(bf16[640,2240]{1,0:T(8,128)(2,1)S(1)} %bitcast.65, bf16[2240,2240]{1,0:T(8,128)(2,1)} %reshape.292), kind=kOutput, calls=%fused_computation.6 | convolution fusion | flops 6423961600 | bytes 15769600 | tf_op jit(solution)/shard_map/dot_general | solution.py:140
  268.0 5.4 %copy.61 = bf16[640,2240]{1,0:T(8,128)(2,1)} copy(bf16[640,2240]{0,1:T(8,128)(2,1)} %convolution_convert_fusion) | data formatting | bytes 5734400 | tf_op jit(solution)/shard_map/convert_element_type | solution.py:145
  (27 shorter events, 0.2 us)
Async XLA Ops:
  6.5 24.9 %copy-start.1 = (bf16[1,8,80,2240]{3,2,1,0:T(8,128)(2,1)S(1)}, bf16[1,8,80,2240]{3,2,1,0:T(8,128)(2,1)}, u32[]{:S(2)}) copy-start(bf16[1,8,80,2240]{3,2,1,0:T(8,128)(2,1)} %param.6) | copy-start | bytes 8601604
  6.5 237.0 %all-gather.7.cloned.1.call-start = ((), (), s32[]{:S(2)}) async-start(), calls=%async_computation.2 | async-start | bytes 10948608 | tf_op jit(solution)/shard_map/all_gather | solution.py:142
  33.2 7.7 %copy-start = (bf16[1,8,80,2240]{3,2,1,0:T(8,128)(2,1)S(1)}, bf16[1,8,80,2240]{3,2,1,0:T(8,128)(2,1)}, u32[]{:S(2)}) copy-start(bf16[1,8,80,2240]{3,2,1,0:T(8,128)(2,1)} %param.7) | copy-start | bytes 8601604
  61.9 45.7 %all-to-all-start = ((f32[8,20,14,113]{3,2,1,0:T(8,128)}), f32[8,20,14,113]{3,2,1,0:T(8,128)}, u32[]{:S(2)}, u32[]{:S(2)}) async-start(f32[8,20,14,113]{3,2,1,0:T(8,128)} %copy.45), calls=%async_computation | async-start | bytes 2621440 | tf_op jit(solution)/shard_map/all_to_all | solution.py:24
  68.3 34.2 %collective-permute-start = (bf16[1,80,2240]{2,1,0:T(8,128)(2,1)}, bf16[1,80,2240]{2,1,0:T(8,128)(2,1)S(1)}, u32[]{:S(2)}, u32[]{:S(2)}) collective-permute-start(bf16[1,80,2240]{2,1,0:T(8,128)(2,1)} %get-tuple-element.14), channel_id=1, source_target_pairs={{0,1},{1,2},{2,3},{3,4},{4,5},{5,6},{6,7},{8,9},{9,10},{10,11},{11... | collective-permute-start | bytes 1075208 | tf_op jit(solution)/shard_map/ppermute | solution.py:80
  71.7 32.0 %collective-permute-start.1 = (bf16[1,80,2240]{2,1,0:T(8,128)(2,1)}, bf16[1,80,2240]{2,1,0:T(8,128)(2,1)}, u32[]{:S(2)}, u32[]{:S(2)}) collective-permute-start(bf16[1,80,2240]{2,1,0:T(8,128)(2,1)} %get-tuple-element.15), channel_id=1, source_target_pairs={{1,0},{2,1},{3,2},{4,3},{5,4},{6,5},{7,6},{9,8},{10,9},{11,10},{12... | collective-permute-start | bytes 1075208 | tf_op jit(solution)/shard_map/ppermute | solution.py:82
  85.6 6.0 %copy-start.4 = (f32[3,3,2240]{2,1,0:T(4,128)S(1)}, f32[3,3,2240]{2,1,0:T(4,128)}, u32[]{:S(2)}) copy-start(f32[3,3,2240]{2,1,0:T(4,128)} %param.8) | copy-start | bytes 241924
  150.8 55.6 %copy-start.2 = (bf16[640,20,112]{0,2,1:T(8,128)(2,1)S(1)}, bf16[640,20,112]{0,2,1:T(8,128)(2,1)}, u32[]{:S(2)}) copy-start(bf16[640,20,112]{0,2,1:T(8,128)(2,1)} %copy.57) | copy-start | bytes 8601604
  220.3 8.7 %copy-start.5 = (f32[2240]{0:T(1024)S(1)}, f32[2240]{0:T(1024)}, u32[]{:S(2)}) copy-start(f32[2240]{0:T(1024)} %get-tuple-element.6) | copy-start | bytes 26884
  220.3 8.7 %copy-start.6 = (f32[2240]{0:T(1024)S(1)}, f32[2240]{0:T(1024)}, u32[]{:S(2)}) copy-start(f32[2240]{0:T(1024)} %get-tuple-element.7) | copy-start | bytes 26884
  220.3 8.7 %copy-start.7 = (f32[2240]{0:T(1024)S(1)}, f32[2240]{0:T(1024)}, u32[]{:S(2)}) copy-start(f32[2240]{0:T(1024)} %get-tuple-element.8) | copy-start | bytes 26884
  220.3 8.7 %copy-start.8 = (f32[2240]{0:T(1024)S(1)}, f32[2240]{0:T(1024)}, u32[]{:S(2)}) copy-start(f32[2240]{0:T(1024)} %get-tuple-element.9) | copy-start | bytes 26884
  220.3 8.7 %copy-start.9 = (f32[2240]{0:T(1024)S(1)}, f32[2240]{0:T(1024)}, u32[]{:S(2)}) copy-start(f32[2240]{0:T(1024)} %get-tuple-element.10) | copy-start | bytes 26884
  220.3 8.7 %copy-start.10 = (f32[2240]{0:T(1024)S(1)}, f32[2240]{0:T(1024)}, u32[]{:S(2)}) copy-start(f32[2240]{0:T(1024)} %get-tuple-element.11) | copy-start | bytes 26884
  220.3 8.7 %copy-start.11 = (f32[2240]{0:T(1024)S(1)}, f32[2240]{0:T(1024)}, u32[]{:S(2)}) copy-start(f32[2240]{0:T(1024)} %get-tuple-element.12) | copy-start | bytes 26884
  220.3 8.7 %copy-start.12 = (f32[2240]{0:T(1024)S(1)}, f32[2240]{0:T(1024)}, u32[]{:S(2)}) copy-start(f32[2240]{0:T(1024)} %get-tuple-element.13) | copy-start | bytes 26884
  243.5 12.3 %copy-start.3 = (bf16[8,80,2240]{2,1,0:T(8,128)(2,1)S(1)}, bf16[8,80,2240]{2,1,0:T(8,128)(2,1)}, u32[]{:S(2)}) copy-start(bf16[8,80,2240]{2,1,0:T(8,128)(2,1)} %add_convert_fusion) | copy-start | bytes 8601604
Sparse Core Ops, SparseCore 0:
  31.6 60.4 all-gather.6
where the time goes:
time: 282 us; the launch traced here: 280 us
  blocking collectives  105 us (37%)
  local copies, waits for them, and re-layouts  83 us (29%)
  other arithmetic  33.3 us (12%)
  matrix products  22.3 us (8%)
  between operations  13.6 us (5%)
  starting transfers between devices  11.4 us (4%)
  waiting for transfers between devices  11.2 us (4%)
    all_gather x6, blocking collectives, entering(): pieces = jax.tree.map(lambda part: lax.all_gather(part, axis), total)  55.8 us
    all_gather x1, blocking collectives, side_by_side_2(): result = lax.all_gather(both, axis, axis=dim, tiled=True)  27 us
    all_to_all x1, blocking collectives, sent_to_all(): lax.all_to_all(jnp.broadcast_to(x[None], (length, *x.shape)), axis, 0, 0,...  22.6 us
    unnamed x32, local copies, waits for them, and re-layouts  18.9 us
    reshape x2, local copies, waits for them, and re-layouts, shards(): (numer / (denom[:, :, None] + epsilon)).reshape(row_count, col_count, fea...  18.4 us
    convert_element_type x1, other arithmetic, shards(): mix = (attn + conv).astype(jnp.bfloat16).reshape(token_count, feature_count)  14.5 us
    reshape x2, local copies, waits for them, and re-layouts, shards(): jnp.maximum(queries, 0).reshape(token_count, head_count, head_size)  13.7 us
    dot_general x1, matrix products, shards(): jnp.dot(mix, lax.all_gather(weight_block, TM, axis=0, tiled=True), prefer...  12.3 us
  transfers between devices with their start and end apart: 4, of which 2 were waited for; matrix products, arithmetic and copies ran while one was open for 38% of the time, Pallas kernels for 0%

commit v1 on v0

v1 whole, which is shorter than its diff:
```python
import functools

import jax
import jax.numpy as jnp
from jax import lax
from jax.experimental import pallas as pl
from jax.experimental.pallas import tpu as pltpu
from jax.sharding import PartitionSpec as P

HEADS = 20
HD = 112
D = HEADS * HD
ROWS, COLS = 8, 80
TOK = ROWS * COLS
LANES = 128
TILES = 18
DP = TILES * LANES
BLK, BLKP = 70, 72
UNITS = 7
NZ = 8
EPS = 1e-06
MESH = pl.DeviceIdType.MESH
F32, BF16 = jnp.float32, jnp.bfloat16


def feature_of(pos):
    return BLK * (pos // BLKP) + min(pos % BLKP, BLK - 1)


def spread_window(j):
    lo = feature_of(LANES * j) // LANES
    lo = min(lo, TILES - 2)
    return lo, LANES * lo, min(LANES * (lo + 2), D)


def spread_matrix(j, start, stop):
    shape = (stop - start, LANES)
    pos = LANES * j + lax.broadcasted_iota(jnp.int32, shape, 1)
    block = lax.shift_right_logical(pos * 14564, 20)
    inside = pos - BLKP * block
    feature = BLK * block + inside
    row = start + lax.broadcasted_iota(jnp.int32, shape, 0)
    return jnp.where((row == feature) & (inside < BLK), 1.0, 0.0).astype(BF16)


def dot(a, b):
    return jnp.dot(a, b, preferred_element_type=F32)


def add_mod(a, b, n):
    return lax.rem(a + b + 2 * n, n)


def gather_kernel(
    k_hbm, v_hbm, w_hbm, cw_ref, conv_hbm, s_hbm, wg_hbm,
    kn, vn, kt, vp, cwp, conv, z_ref, fwd, bwd, own, scan, pre, xs, back, s_own, wa, wown,
    local_sem, halo_send, halo_recv, wa_send, wa_recv, rs_send, rs_recv, sc_send, sc_recv,
    xs_send, xs_recv, bk_send, bk_recv, ag_send, ag_recv, wg_send, wg_recv,
):
    tm, z = lax.axis_index("tm"), lax.axis_index("space")
    core, y, x = lax.rem(tm, 2), lax.rem(lax.div(tm, 2), 4), lax.div(tm, 8)
    member = lax.rem(tm, 8)
    dr = 1 - 2 * core

    def at(xx, yy, cc):
        return 8 * xx + 2 * yy + cc

    def along_a(k):
        other = add_mod(jnp.where(core == 0, x, y), k, 4)
        return jnp.where(core == 0, at(other, y, core), at(x, other, core))

    def along(ka, kb):
        px = add_mod(x, jnp.where(core == 0, ka, kb), 4)
        py = add_mod(y, jnp.where(core == 0, kb, ka), 4)
        return at(px, py, core)

    partner = at(x, y, 1 - core)
    everything = []

    def remote(src, dst, send, recv, to_tm, to_z):
        return pltpu.make_async_remote_copy(
            src_ref=src, dst_ref=dst, send_sem=send, recv_sem=recv,
            device_id={"tm": to_tm, "space": to_z}, device_id_type=MESH,
        )

    def start(copy):
        copy.start()
        everything.append(copy)
        return copy

    barrier = pltpu.get_barrier_semaphore()
    friends = [(tm, add_mod(z, o, NZ)) for o in range(1, NZ)]
    friends += [(8 * x + add_mod(member, o, 8), z) for o in range(1, 8)]
    friends += [(add_mod(tm, 8 * o, 32), z) for o in range(1, 4)]
    for to_tm, to_z in friends:
        pl.semaphore_signal(barrier, inc=1, device_id={"tm": to_tm, "space": to_z}, device_id_type=MESH)
    loads = [
        pltpu.make_async_copy(k_hbm, kn, local_sem.at[0]),
        pltpu.make_async_copy(v_hbm, vn.at[pl.ds(COLS, TOK)], local_sem.at[1]),
    ]
    for copy in loads:
        copy.start()
    pl.semaphore_wait(barrier, len(friends))

    wa_mine = pltpu.make_async_copy(w_hbm, wa.at[z], local_sem.at[2])
    wa_mine.start()
    for o in range(1, NZ):
        start(remote(w_hbm, wa.at[z], wa_send.at[o - 1], wa_recv.at[o - 1], tm, add_mod(z, o, NZ)))
    halo = [
        remote(v_hbm.at[pl.ds(0, COLS)], vn.at[pl.ds(COLS + TOK, COLS)], halo_send.at[0], halo_recv.at[0], tm, add_mod(z, -1, NZ)),
        remote(v_hbm.at[pl.ds(TOK - COLS, COLS)], vn.at[pl.ds(0, COLS)], halo_send.at[1], halo_recv.at[1], tm, add_mod(z, 1, NZ)),
    ]
    for copy in halo:
        start(copy)

    def partial_state():
        loads[0].wait()
        for i in range(TILES):
            lo, hi = LANES * i, min(LANES * (i + 1), D)
            kt[lo:hi, :] = jnp.maximum(kn[:, lo:hi], 0).T
        loads[1].wait()
        ones = jnp.ones((TOK, LANES), BF16)
        lane = lax.broadcasted_iota(jnp.int32, (HD, LANES), 1)
        sums = jnp.zeros((HD, LANES), F32)
        for j in range(TILES):
            lo, hi = LANES * j, min(LANES * (j + 1), D)
            tile = vn[COLS : COLS + TOK, lo:hi]
            if hi - lo < LANES:
                eye = lax.broadcasted_iota(jnp.int32, (hi - lo, LANES), 0) == lax.broadcasted_iota(jnp.int32, (hi - lo, LANES), 1)
                tile = dot(tile, jnp.where(eye, 1.0, 0.0).astype(BF16)).astype(BF16)
            first, last = lo // HD, (hi - 1) // HD
            g = dot(kt[HD * first : HD * (last + 1), :], jnp.concatenate([tile, ones], axis=1))
            part = g[:HD, :LANES]
            for h in range(first, last + 1):
                rows = g[HD * (h - first) : HD * (h - first + 1)]
                part = jnp.where(lane < HD * h - lo, part, rows[:, :LANES])
                sums = jnp.where(lane == D - LANES * (TILES - 1) + h, rows[:, LANES:], sums)
            if j == TILES - 1:
                part = jnp.where(lane < D - lo, part, sums)
            for r in range(UNITS):
                z_ref[UNITS * j + r] = part[16 * r : 16 * (r + 1)]
        z_ref[UNITS * TILES] = jnp.zeros((16, LANES), F32)
        z_ref[UNITS * TILES + 1] = jnp.zeros((16, LANES), F32)

    def ring(forward, s, u):
        hops = 4 if forward else 3
        way = dr if forward else -dr
        slots = fwd if forward else bwd
        chunk = add_mod(z, way * (hops - s), NZ)
        place = pl.ds(8 * u, 8)
        sem = (0 if forward else 8) + 2 * s + u
        if s == 0:
            src = z_ref.at[pl.ds(16 * chunk + 8 * u, 8)]
        else:
            everything_rs[(forward, s - 1, u)].wait_recv()
            slots[s - 1, place] += z_ref[pl.ds(16 * chunk + 8 * u, 8)]
            src = slots.at[s - 1, place]
        copy = remote(src, slots.at[s, place], rs_send.at[sem], rs_recv.at[sem], tm, add_mod(z, way, NZ))
        copy.start()
        everything_rs[(forward, s, u)] = copy

    everything_rs = {}

    def ring_step(s):
        for u in range(2):
            ring(True, s, u)
            if s < 3:
                ring(False, s, u)

    def ring_end():
        for u in range(2):
            everything_rs[(True, 3, u)].wait_recv()
            everything_rs[(False, 2, u)].wait_recv()
            place = pl.ds(8 * u, 8)
            own[place] = z_ref[pl.ds(16 * z + 8 * u, 8)] + fwd[3, place] + bwd[2, place]

    def scan_send():
        for o in range(1, 8):
            other = add_mod(member, o, 8)
            start(remote(own.at[pl.ds(2 * other, 2)], scan.at[member], sc_send.at[o - 1], sc_recv.at[o - 1], 8 * x + other, z))
        scan[member] = own[pl.ds(2 * member, 2)]

    def scan_group():
        for o in range(1, 8):
            remote(own.at[pl.ds(0, 2)], scan.at[0], sc_send.at[o - 1], sc_recv.at[o - 1], tm, z).wait_recv()
        total = jnp.zeros((2, 16, LANES), F32)
        for m in range(8):
            total = total + scan[m]
            pre[m] = total
        for o in range(1, 4):
            start(remote(pre.at[7], xs.at[x], xs_send.at[o - 1], xs_recv.at[o - 1], add_mod(tm, 8 * o, 32), z))
        xs[x] = total

    def scan_back():
        for o in range(1, 4):
            remote(pre.at[7], xs.at[0], xs_send.at[o - 1], xs_recv.at[o - 1], tm, z).wait_recv()
        before = jnp.zeros((2, 16, LANES), F32)
        for k in range(4):
            before = before + jnp.where(k < x, xs[k], 0.0)
        for m in range(8):
            back[m] = (before + pre[m]).astype(BF16)
        for o in range(1, 8):
            other = add_mod(member, o, 8)
            start(remote(back.at[other], s_own.at[pl.ds(2 * member, 2)], bk_send.at[o - 1], bk_recv.at[o - 1], 8 * x + other, z))
        s_own[pl.ds(2 * member, 2)] = back[member]

    def share_state():
        for o in range(1, 8):
            remote(back.at[0], s_own.at[pl.ds(0, 2)], bk_send.at[o - 1], bk_recv.at[o - 1], tm, z).wait_recv()
        dst = s_hbm.at[pl.ds(16 * z, 16)]
        for o in range(1, NZ):
            start(remote(s_own, dst, ag_send.at[o - 1], ag_recv.at[o - 1], tm, add_mod(z, o, NZ)))
        copy = pltpu.make_async_copy(s_own, dst, local_sem.at[3])
        copy.start()
        return copy

    def rows_of(owner, half=None):
        lo, n = (0, BLKP) if half is None else ((0, 40) if half == 0 else (40, 32))
        return wg_hbm.at[pl.ds(pl.multiple_of(BLKP * owner + lo, 8), n)]

    def w_send(n, src, dst, to_tm):
        start(remote(src, dst, wg_send.at[n], wg_recv.at[n], to_tm, z))

    def w_wait(n, ref):
        remote(ref, ref, wg_send.at[n], wg_recv.at[n], tm, z).wait_recv()

    deltas = (0, -1, 1, 2)

    def w_out_b(g, src=None):
        owner = along(deltas[g], 0)
        ref = rows_of(owner) if src is None else src
        w_send(4 + 4 * g, ref, rows_of(owner), along(0, 1))
        w_send(5 + 4 * g, ref, rows_of(owner), along(0, -1))
        w_send(20 + 4 * g, ref, rows_of(owner), partner)

    def w_assemble():
        wa_mine.wait()
        for o in range(1, NZ):
            remote(w_hbm, wa.at[0], wa_send.at[o - 1], wa_recv.at[o - 1], tm, z).wait_recv()
        wown[...] = jnp.zeros((BLKP, DP), BF16)
        width = D // NZ
        for j in range(TILES):
            lo, hi = LANES * j, min(LANES * (j + 1), D)
            acc = jnp.zeros((BLK, LANES), F32)
            for b in range(lo // width, (hi - 1) // width + 1):
                row = width * b + lax.broadcasted_iota(jnp.int32, (width, LANES), 0)
                col = lo + lax.broadcasted_iota(jnp.int32, (width, LANES), 1)
                acc = acc + dot(wa[b], jnp.where(row == col, 1.0, 0.0).astype(BF16))
            wown[0:BLK, lo : lo + LANES] = acc.astype(BF16)
        mine = pltpu.make_async_copy(wown, rows_of(tm), local_sem.at[4])
        mine.start()
        w_send(0, wown, rows_of(tm), along(1, 0))
        w_send(1, wown, rows_of(tm), along(-1, 0))
        w_out_b(0, wown)
        return mine

    def w_a_full():
        low, high = along(-1, 0), along(1, 0)
        w_wait(0, rows_of(low))
        w_send(2, rows_of(low, 0), rows_of(low, 0), high)
        w_out_b(1)
        w_wait(1, rows_of(high))
        w_send(3, rows_of(high, 1), rows_of(high, 1), low)
        w_out_b(2)

    def w_a_half():
        w_wait(2, rows_of(along(2, 0), 0))
        w_wait(3, rows_of(along(2, 0), 1))
        w_out_b(3)

    def w_b_full(g):
        low, high = along(deltas[g], -1), along(deltas[g], 1)
        w_wait(4 + 4 * g, rows_of(low))
        w_send(6 + 4 * g, rows_of(low, 0), rows_of(low, 0), along(0, 1))
        w_send(21 + 4 * g, rows_of(low), rows_of(low), partner)
        w_wait(5 + 4 * g, rows_of(high))
        w_send(7 + 4 * g, rows_of(high, 1), rows_of(high, 1), along(0, -1))
        w_send(22 + 4 * g, rows_of(high), rows_of(high), partner)

    def w_b_half(g):
        far = along(deltas[g], 2)
        w_wait(6 + 4 * g, rows_of(far, 0))
        w_wait(7 + 4 * g, rows_of(far, 1))
        w_send(23 + 4 * g, rows_of(far), rows_of(far), partner)

    def w_end():
        for n in range(20, 36):
            w_wait(n, rows_of(0))

    def conv_prepare():
        for copy in halo:
            copy.wait_recv()

        @pl.when(z == 0)
        def _():
            vn[0:COLS, :] = jnp.zeros((COLS, D), BF16)

        @pl.when(z == NZ - 1)
        def _():
            vn[COLS + TOK :, :] = jnp.zeros((COLS, D), BF16)

        for j in range(TILES):
            _, lo, hi = spread_window(j)
            spread = spread_matrix(j, lo, hi)
            place = slice(LANES * j, LANES * (j + 1))
            vp[:, place] = dot(vn[:, lo:hi], spread).astype(BF16)
            for a in range(3):
                rest = cw_ref[a, :, lo:hi]
                total = jnp.zeros((3, LANES), F32)
                for _ in range(3):
                    piece = rest.astype(BF16)
                    total = total + dot(piece, spread)
                    rest = rest - piece.astype(F32)
                cwp[a, 0:3, place] = total

    def conv_rows(first, last):
        row = lax.broadcasted_iota(jnp.int32, (COLS, LANES), 0)

        @pl.loop(first, last)
        def _(r):
            base = pl.multiple_of(COLS * r, 16)
            for j in range(TILES):
                place = slice(LANES * j, LANES * (j + 1))
                lines = [vp[pl.ds(base + COLS * a, COLS), place].astype(F32) for a in range(3)]
                sums = []
                for b in range(3):
                    sums.append(sum(lines[a] * cwp[a, b : b + 1, place] for a in range(3)))
                left = jnp.where(row == 0, 0.0, pltpu.roll(sums[0], 1, 0))
                right = jnp.where(row == COLS - 1, 0.0, pltpu.roll(sums[2], COLS - 1, 0))
                conv[pl.ds(base, COLS), place] = sums[1] + left + right

    partial_state()
    ring_step(0)
    mine = w_assemble()
    conv_prepare()
    ring_step(1)
    conv_rows(0, 2)
    ring_step(2)
    w_a_full()
    conv_rows(2, 5)
    ring_step(3)
    w_b_full(0)
    conv_rows(5, 8)
    conv_out = pltpu.make_async_copy(conv, conv_hbm, local_sem.at[5])
    conv_out.start()
    ring_end()
    scan_send()
    w_a_half()
    scan_group()
    mine.wait()
    scan_back()
    w_b_full(1)
    state_mine = share_state()
    w_b_full(2)
    w_b_half(0)
    w_b_full(3)
    w_b_half(1)
    w_b_half(2)
    w_b_half(3)
    for o in range(1, NZ):
        remote(s_own, s_hbm.at[pl.ds(0, 16)], ag_send.at[o - 1], ag_recv.at[o - 1], tm, z).wait_recv()
    w_end()
    for copy in everything + list(everything_rs.values()):
        copy.wait_send()
    state_mine.wait()
    conv_out.wait()


def gather(k, v, w, cw):
    dma = pltpu.SemaphoreType.DMA
    any_space = pl.BlockSpec(memory_space=pl.ANY)
    return pl.pallas_call(
        gather_kernel,
        out_shape=(
            jax.ShapeDtypeStruct((TOK, DP), F32),
            jax.ShapeDtypeStruct((16 * NZ, 16, LANES), BF16),
            jax.ShapeDtypeStruct((32 * BLKP, DP), BF16),
        ),
        in_specs=[any_space, any_space, any_space, pl.BlockSpec(memory_space=pltpu.VMEM)],
        out_specs=(any_space,) * 3,
        scratch_shapes=[
            pltpu.VMEM((TOK, D), BF16),
            pltpu.VMEM((TOK + 2 * COLS, D), BF16),
            pltpu.VMEM((D, TOK), BF16),
            pltpu.VMEM((TOK + 2 * COLS, DP), BF16),
            pltpu.VMEM((3, 8, DP), F32),
            pltpu.VMEM((TOK, DP), F32),
            pltpu.VMEM((16 * NZ, 16, LANES), F32),
            pltpu.VMEM((4, 16, 16, LANES), F32),
            pltpu.VMEM((3, 16, 16, LANES), F32),
            pltpu.VMEM((16, 16, LANES), F32),
            pltpu.VMEM((8, 2, 16, LANES), F32),
            pltpu.VMEM((8, 2, 16, LANES), F32),
            pltpu.VMEM((4, 2, 16, LANES), F32),
            pltpu.VMEM((8, 2, 16, LANES), BF16),
            pltpu.VMEM((16, 16, LANES), BF16),
            pltpu.VMEM((NZ, BLK, D // NZ), BF16),
            pltpu.VMEM((BLKP, DP), BF16),
            dma((6,)), dma((2,)), dma((2,)), dma((7,)), dma((7,)), dma((14,)), dma((14,)),
            dma((7,)), dma((7,)), dma((3,)), dma((3,)), dma((7,)), dma((7,)), dma((7,)), dma((7,)),
            dma((36,)), dma((36,)),
        ],
        compiler_params=pltpu.CompilerParams(
            collective_id=0, has_side_effects=True, vmem_limit_bytes=48 << 20
        ),
        name="state_and_gather",
    )(k, v, w, cw)


def heads_of(j):
    features = [
        feature_of(p) for p in range(LANES * j, LANES * (j + 1)) if p % BLKP < BLK
    ]
    first, last = min(features) // HD, max(features) // HD
    lo = HD * first // LANES * LANES
    hi = min(-(-HD * (last + 1) // LANES) * LANES, D)
    return first, last, lo, hi


def project_kernel(q_hbm, conv_hbm, s_hbm, w_hbm, out_ref, qv, cv, sv, sn, band, mix, wv, sem):
    n = pl.program_id(0)
    steps = DP // 256
    copies = [
        pltpu.make_async_copy(s_hbm, sv, sem.at[0]),
        pltpu.make_async_copy(q_hbm, qv, sem.at[1]),
        pltpu.make_async_copy(conv_hbm, cv, sem.at[2]),
    ]
    weights = [
        pltpu.make_async_copy(
            w_hbm.at[:, pl.ds(256 * t, 256)], wv.at[:, pl.ds(256 * t, 256)], sem.at[3 + t]
        )
        for t in range(steps)
    ]

    @pl.when(n == 0)
    def _():
        for copy in copies + weights:
            copy.start()
        copies[0].wait()
        for j in range(TILES):
            for r in range(UNITS):
                sn[16 * r : 16 * (r + 1), LANES * j : LANES * (j + 1)] = sv[UNITS * j + r]
        sums = sn[:, LANES * (TILES - 1) :]
        base = D - LANES * (TILES - 1)
        for j in range(TILES):
            first, last, lo, hi = heads_of(j)
            band[j] = jnp.zeros(band.shape[1:], BF16)
            _, w_lo, _ = spread_window(j)
            w_hi = w_lo + 2 * LANES
            spread = spread_matrix(j, w_lo, w_hi)
            state = dot(sn[:, w_lo:w_hi], spread).astype(BF16)
            pos = LANES * j + lax.broadcasted_iota(jnp.int32, (LANES, LANES), 1)
            block = lax.shift_right_logical(pos * 14564, 20)
            inside = pos - BLKP * block
            feature = BLK * block + inside
            row = lax.broadcasted_iota(jnp.int32, (LANES, LANES), 0)
            for h in range(first, last + 1):
                member = (inside < BLK) & (feature >= HD * h) & (feature < HD * (h + 1))
                pick = jnp.where(member & (row == base + h), 1.0, 0.0).astype(BF16)
                keep = jnp.where(member[:1], 1.0, 0.0).astype(BF16)
                at = slice(HD * h - lo, HD * (h + 1) - lo)
                band[j, at, :LANES] = state * keep
                band[j, at, LANES:] = dot(sums, pick).astype(BF16)
        copies[1].wait()
        qv[...] = jnp.maximum(qv[...], 0)
        copies[2].wait()
        for j in range(TILES):
            _, _, lo, hi = heads_of(j)
            place = slice(LANES * j, LANES * (j + 1))
            both = dot(qv[:, lo:hi], band[j, : hi - lo, :])
            attn = both[:, :LANES] / (both[:, LANES:] + EPS)
            mix[:, place] = (attn + cv[:, place]).astype(BF16)

    for t in range(steps):

        @pl.when(n == t)
        def _():
            weights[t].wait()

    at = pl.ds(pl.multiple_of(256 * n, 256), 256)
    out_ref[...] = dot(mix[...], wv[:, at]).astype(BF16)


def project(q, conv, s, w):
    any_space = pl.BlockSpec(memory_space=pl.ANY)
    return pl.pallas_call(
        project_kernel,
        grid=(DP // 256,),
        out_shape=jax.ShapeDtypeStruct((TOK, D), BF16),
        in_specs=[any_space] * 4,
        out_specs=pl.BlockSpec((TOK, 256), lambda n: (0, n)),
        scratch_shapes=[
            pltpu.VMEM((TOK, D), BF16),
            pltpu.VMEM((TOK, DP), F32),
            pltpu.VMEM((16 * NZ, 16, LANES), BF16),
            pltpu.VMEM((HD, DP), BF16),
            pltpu.VMEM((TILES, 512, 256), BF16),
            pltpu.VMEM((TOK, DP), BF16),
            pltpu.VMEM((32 * BLKP, DP), BF16),
            pltpu.SemaphoreType.DMA((3 + DP // 256,)),
        ],
        compiler_params=pltpu.CompilerParams(vmem_limit_bytes=48 << 20),
        name="attend_and_project",
    )(q, conv, s, w)


def shards(queries, keys, values, conv_weight, w_out):
    q, k, v = (a.reshape(TOK, D) for a in (queries, keys, values))
    conv, states, weights = gather(k, v, w_out, conv_weight)
    return project(q, conv, states, weights).reshape(1, ROWS, COLS, D)


def solution(mesh):
    placed = P("tm", "space", None, None)
    return jax.shard_map(
        shards,
        mesh=mesh,
        in_specs=(placed, placed, placed, P(), P("tm", "space")),
        out_specs=placed,
        check_vma=False,
    )
```

time: 282 us -> 93.8 us (0.33)
  the two profiles are of different devices: /device:TPU:32 before, /device:TPU:1 now
where the time goes in v1:
time: 93.8 us; the launch traced here: 93.6 us
  Pallas kernels  89.9 us (96%)
  local copies, waits for them, and re-layouts  3.55 us (4%)
    pallas_call x1, Pallas kernels, gather(): pl.pallas_call(gather_kernel, out_shape=(jax.ShapeDtypeStruct((TOK, DP),...  74.8 us
    pallas_call x1, Pallas kernels, project(): pl.pallas_call(project_kernel, grid=(DP // 256,), out_shape=jax.ShapeDtyp...  15.1 us
    unnamed x8, local copies, waits for them, and re-layouts  3.55 us

profile of v1, /device:TPU:1, one launch (start us, length us, event | category | flops | bytes accessed | tf_op | source)
XLA Modules:
  0.0 93.6 jit_solution(16465707566579211450)
XLA Ops:
  0.0 0.0 copy-start
  0.0 1.8 %copy-done = bf16[1,8,80,2240]{3,2,1,0:T(8,128)(2,1)S(1)} copy-done((bf16[1,8,80,2240]{3,2,1,0:T(8,128)(2,1)S(1)}, bf16[1,8,80,2240]{3,2,1,0:T(8,128)(2,1)}, u32[]{:S(2)}) %copy-start) | copy-done | bytes 2867224
  1.8 0.0 copy-start.2
  1.8 0.9 copy-done.2
  2.7 0.0 copy-start.3
  2.7 0.8 copy-done.3
  3.5 0.0 copy-start.1
  3.5 74.8 %state_and_gather.1 = (f32[640,2304]{1,0:T(8,128)}, bf16[128,16,128]{2,1,0:T(8,128)(2,1)S(1)}, bf16[2304,2304]{1,0:T(8,128)(2,1)}) custom-call(bf16[640,2240]{1,0:T(8,128)(2,1)S(1)} %bitcast.4, bf16[640,2240]{1,0:T(8,128)(2,1)} %bitcast.6, bf16[70,280]{1,0:T(8,128)(2,1)S(1)} %copy-done.3, f32[3,3,2240]{2,1,0:T(4,128)S(1)} %copy-done.2), custom_call_target="tpu_custom_call" | custom-call | tf_op jit(solution)/shard_map/state_and_gather/pallas_call | solution.py:372
  78.4 0.0 copy-done.1
  78.4 15.1 %attend_and_project.1 = bf16[640,2240]{1,0:T(8,128)(2,1)} custom-call(bf16[640,2240]{1,0:T(8,128)(2,1)S(1)} %bitcast.5, f32[640,2304]{1,0:T(8,128)} %get-tuple-element.8.conv_hbm, bf16[128,16,128]{2,1,0:T(8,128)(2,1)S(1)} %get-tuple-element.9.s_hbm, bf16[2304,2304]{1,0:T(8,128)(2,1)} %get-tuple-element.10.w_hbm), custom_call_target="tpu_custom_call" | custom-call | tf_op jit(solution)/shard_map/attend_and_project/pallas_call | solution.py:486
Async XLA Ops:
  0.0 1.8 %copy-start = (bf16[1,8,80,2240]{3,2,1,0:T(8,128)(2,1)S(1)}, bf16[1,8,80,2240]{3,2,1,0:T(8,128)(2,1)}, u32[]{:S(2)}) copy-start(bf16[1,8,80,2240]{3,2,1,0:T(8,128)(2,1)} %param.6) | copy-start | bytes 8601604
  1.8 0.9 copy-start.2
  2.7 0.8 copy-start.3
  3.5 74.8 %copy-start.1 = (bf16[1,8,80,2240]{3,2,1,0:T(8,128)(2,1)S(1)}, bf16[1,8,80,2240]{3,2,1,0:T(8,128)(2,1)}, u32[]{:S(2)}) copy-start(bf16[1,8,80,2240]{3,2,1,0:T(8,128)(2,1)} %param.5) | copy-start | bytes 8601604

commit v2 on v1

--- a/solution.py
+++ b/solution.py
@@ -19,6 +19,8 @@
 UNITS = 7
 NZ = 8
 EPS = 1e-06
+SUBS = 4
+PART = 16 // SUBS
 MESH = pl.DeviceIdType.MESH
 F32, BF16 = jnp.float32, jnp.bfloat16
 
@@ -52,8 +54,8 @@
 
 
 def gather_kernel(
-    k_hbm, v_hbm, w_hbm, cw_ref, conv_hbm, s_hbm, wg_hbm,
-    kn, vn, kt, vp, cwp, conv, z_ref, fwd, bwd, own, scan, pre, xs, back, s_own, wa, wown,
+    k_hbm, v_hbm, w_hbm, cw_hbm, conv_hbm, s_hbm, wg_hbm,
+    cw_ref, kn, vn, kt, vp, cwp, conv, z_ref, fwd, bwd, own, scan, pre, xs, back, s_own, wa, wown,
     local_sem, halo_send, halo_recv, wa_send, wa_recv, rs_send, rs_recv, sc_send, sc_recv,
     xs_send, xs_recv, bk_send, bk_recv, ag_send, ag_recv, wg_send, wg_recv,
 ):
@@ -98,20 +100,20 @@
         pltpu.make_async_copy(k_hbm, kn, local_sem.at[0]),
         pltpu.make_async_copy(v_hbm, vn.at[pl.ds(COLS, TOK)], local_sem.at[1]),
     ]
+    load_cw = pltpu.make_async_copy(cw_hbm, cw_ref, local_sem.at[6])
     for copy in loads:
         copy.start()
     pl.semaphore_wait(barrier, len(friends))
 
     wa_mine = pltpu.make_async_copy(w_hbm, wa.at[z], local_sem.at[2])
     wa_mine.start()
-    for o in range(1, NZ):
-        start(remote(w_hbm, wa.at[z], wa_send.at[o - 1], wa_recv.at[o - 1], tm, add_mod(z, o, NZ)))
+    load_cw.start()
+    for n, o in enumerate((1, -1, 2, -2)):
+        start(remote(w_hbm, wa.at[z], wa_send.at[n], wa_recv.at[n], tm, add_mod(z, o, NZ)))
     halo = [
         remote(v_hbm.at[pl.ds(0, COLS)], vn.at[pl.ds(COLS + TOK, COLS)], halo_send.at[0], halo_recv.at[0], tm, add_mod(z, -1, NZ)),
         remote(v_hbm.at[pl.ds(TOK - COLS, COLS)], vn.at[pl.ds(0, COLS)], halo_send.at[1], halo_recv.at[1], tm, add_mod(z, 1, NZ)),
     ]
-    for copy in halo:
-        start(copy)
 
     def partial_state():
         loads[0].wait()
@@ -147,13 +149,13 @@
         way = dr if forward else -dr
         slots = fwd if forward else bwd
         chunk = add_mod(z, way * (hops - s), NZ)
-        place = pl.ds(8 * u, 8)
-        sem = (0 if forward else 8) + 2 * s + u
+        place = pl.ds(PART * u, PART)
+        sem = (0 if forward else 4 * SUBS) + SUBS * s + u
         if s == 0:
-            src = z_ref.at[pl.ds(16 * chunk + 8 * u, 8)]
+            src = z_ref.at[pl.ds(16 * chunk + PART * u, PART)]
         else:
             everything_rs[(forward, s - 1, u)].wait_recv()
-            slots[s - 1, place] += z_ref[pl.ds(16 * chunk + 8 * u, 8)]
+            slots[s - 1, place] += z_ref[pl.ds(16 * chunk + PART * u, PART)]
             src = slots.at[s - 1, place]
         copy = remote(src, slots.at[s, place], rs_send.at[sem], rs_recv.at[sem], tm, add_mod(z, way, NZ))
         copy.start()
@@ -162,17 +164,17 @@
     everything_rs = {}
 
     def ring_step(s):
-        for u in range(2):
+        for u in range(SUBS):
             ring(True, s, u)
             if s < 3:
                 ring(False, s, u)
 
     def ring_end():
-        for u in range(2):
+        for u in range(SUBS):
             everything_rs[(True, 3, u)].wait_recv()
             everything_rs[(False, 2, u)].wait_recv()
-            place = pl.ds(8 * u, 8)
-            own[place] = z_ref[pl.ds(16 * z + 8 * u, 8)] + fwd[3, place] + bwd[2, place]
+            place = pl.ds(PART * u, PART)
+            own[place] = z_ref[pl.ds(16 * z + PART * u, PART)] + fwd[3, place] + bwd[2, place]
 
     def scan_send():
         for o in range(1, 8):
@@ -207,12 +209,40 @@
     def share_state():
         for o in range(1, 8):
             remote(back.at[0], s_own.at[pl.ds(0, 2)], bk_send.at[o - 1], bk_recv.at[o - 1], tm, z).wait_recv()
-        dst = s_hbm.at[pl.ds(16 * z, 16)]
-        for o in range(1, NZ):
-            start(remote(s_own, dst, ag_send.at[o - 1], ag_recv.at[o - 1], tm, add_mod(z, o, NZ)))
-        copy = pltpu.make_async_copy(s_own, dst, local_sem.at[3])
+        for h in range(2):
+            for o in (1, -1, 2, -2):
+                state_send(share_number[o] + h, s_own.at[pl.ds(8 * h, 8)], part_of(0, h), o)
+        copy = pltpu.make_async_copy(s_own, s_hbm.at[pl.ds(16 * z, 16)], local_sem.at[3])
         copy.start()
         return copy
+
+    share_number = {1: 0, -1: 2, 2: 4, -2: 6}
+
+    def part_of(o, h):
+        return s_hbm.at[pl.ds(16 * add_mod(z, o, NZ) + 8 * h, 8)]
+
+    def state_send(n, src, dst, o):
+        start(remote(src, dst, ag_send.at[n], ag_recv.at[n], tm, add_mod(z, o, NZ)))
+
+    def state_wait(n, ref):
+        remote(ref, ref, ag_send.at[n], ag_recv.at[n], tm, z).wait_recv()
+
+    def pass_on_state():
+        for h in range(2):
+            state_wait(4 + h, part_of(-2, h))
+            state_send(8 + h, part_of(-2, h), part_of(-2, h), 1)
+            if h == 0:
+                state_send(12, part_of(-2, 0), part_of(-2, 0), 2)
+            state_wait(6 + h, part_of(2, h))
+            state_send(10 + h, part_of(2, h), part_of(2, h), -1)
+            if h == 1:
+                state_send(13, part_of(2, 1), part_of(2, 1), -2)
+
+    def state_end():
+        for n, (o, h) in {0: (-1, 0), 1: (-1, 1), 2: (1, 0), 3: (1, 1)}.items():
+            state_wait(n, part_of(o, h))
+        for n, (o, h) in {8: (-3, 0), 9: (-3, 1), 10: (3, 0), 11: (3, 1), 12: (4, 0), 13: (4, 1)}.items():
+            state_wait(n, part_of(o, h))
 
     def rows_of(owner, half=None):
         lo, n = (0, BLKP) if half is None else ((0, 40) if half == 0 else (40, 32))
@@ -233,10 +263,21 @@
         w_send(5 + 4 * g, ref, rows_of(owner), along(0, -1))
         w_send(20 + 4 * g, ref, rows_of(owner), partner)
 
+    def wa_wait(n):
+        remote(w_hbm, wa.at[0], wa_send.at[n], wa_recv.at[n], tm, z).wait_recv()
+
+    def wa_pass_on():
+        wa_wait(2)
+        wa_wait(3)
+        below, above = add_mod(z, -2, NZ), add_mod(z, 2, NZ)
+        far = add_mod(z, -2 * dr, NZ)
+        for n, slot, to in ((4, below, add_mod(z, 1, NZ)), (5, above, add_mod(z, -1, NZ)), (6, far, add_mod(z, 2 * dr, NZ))):
+            start(remote(wa.at[slot], wa.at[slot], wa_send.at[n], wa_recv.at[n], tm, to))
+
     def w_assemble():
         wa_mine.wait()
-        for o in range(1, NZ):
-            remote(w_hbm, wa.at[0], wa_send.at[o - 1], wa_recv.at[o - 1], tm, z).wait_recv()
+        for n in (0, 1, 4, 5, 6):
+            wa_wait(n)
         wown[...] = jnp.zeros((BLKP, DP), BF16)
         width = D // NZ
         for j in range(TILES):
@@ -251,30 +292,26 @@
         mine.start()
         w_send(0, wown, rows_of(tm), along(1, 0))
         w_send(1, wown, rows_of(tm), along(-1, 0))
-        w_out_b(0, wown)
         return mine
 
-    def w_a_full():
+    def w_pass_full():
         low, high = along(-1, 0), along(1, 0)
         w_wait(0, rows_of(low))
+        w_wait(1, rows_of(high))
         w_send(2, rows_of(low, 0), rows_of(low, 0), high)
-        w_out_b(1)
-        w_wait(1, rows_of(high))
         w_send(3, rows_of(high, 1), rows_of(high, 1), low)
-        w_out_b(2)
-
-    def w_a_half():
+
+    def w_wait_half():
         w_wait(2, rows_of(along(2, 0), 0))
         w_wait(3, rows_of(along(2, 0), 1))
-        w_out_b(3)
 
     def w_b_full(g):
         low, high = along(deltas[g], -1), along(deltas[g], 1)
         w_wait(4 + 4 * g, rows_of(low))
         w_send(6 + 4 * g, rows_of(low, 0), rows_of(low, 0), along(0, 1))
-        w_send(21 + 4 * g, rows_of(low), rows_of(low), partner)
         w_wait(5 + 4 * g, rows_of(high))
         w_send(7 + 4 * g, rows_of(high, 1), rows_of(high, 1), along(0, -1))
+        w_send(21 + 4 * g, rows_of(low), rows_of(low), partner)
         w_send(22 + 4 * g, rows_of(high), rows_of(high), partner)
 
     def w_b_half(g):
@@ -288,22 +325,12 @@
             w_wait(n, rows_of(0))
 
     def conv_prepare():
-        for copy in halo:
-            copy.wait_recv()
-
-        @pl.when(z == 0)
-        def _():
-            vn[0:COLS, :] = jnp.zeros((COLS, D), BF16)
-
-        @pl.when(z == NZ - 1)
-        def _():
-            vn[COLS + TOK :, :] = jnp.zeros((COLS, D), BF16)
-
+        load_cw.wait()
         for j in range(TILES):
             _, lo, hi = spread_window(j)
             spread = spread_matrix(j, lo, hi)
             place = slice(LANES * j, LANES * (j + 1))
-            vp[:, place] = dot(vn[:, lo:hi], spread).astype(BF16)
+            vp[COLS : COLS + TOK, place] = dot(vn[COLS : COLS + TOK, lo:hi], spread).astype(BF16)
             for a in range(3):
                 rest = cw_ref[a, :, lo:hi]
                 total = jnp.zeros((3, LANES), F32)
@@ -312,6 +339,16 @@
                     total = total + dot(piece, spread)
                     rest = rest - piece.astype(F32)
                 cwp[a, 0:3, place] = total
+
+    def conv_rims():
+        for copy in halo:
+            copy.wait_recv()
+        for n, start_row in enumerate((0, COLS + TOK)):
+            there = jnp.where(z == (0, NZ - 1)[n], 0.0, 1.0)
+            for j in range(TILES):
+                _, lo, hi = spread_window(j)
+                rim = dot(vn[start_row : start_row + COLS, lo:hi], spread_matrix(j, lo, hi))
+                vp[start_row : start_row + COLS, LANES * j : LANES * (j + 1)] = (rim * there).astype(BF16)
 
     def conv_rows(first, last):
         row = lax.broadcasted_iota(jnp.int32, (COLS, LANES), 0)
@@ -331,34 +368,44 @@
 
     partial_state()
     ring_step(0)
-    mine = w_assemble()
+    wa_pass_on()
     conv_prepare()
     ring_step(1)
-    conv_rows(0, 2)
     ring_step(2)
-    w_a_full()
-    conv_rows(2, 5)
+    mine = w_assemble()
     ring_step(3)
+    for copy in halo:
+        start(copy)
+    w_out_b(0, wown)
+    conv_rows(1, 4)
+    ring_end()
+    scan_send()
+    w_pass_full()
+    conv_rows(4, 6)
+    scan_group()
+    w_out_b(1)
     w_b_full(0)
-    conv_rows(5, 8)
+    conv_rows(6, 7)
+    scan_back()
+    w_out_b(2)
+    state_mine = share_state()
+    w_wait_half()
+    w_out_b(3)
+    conv_rims()
+    conv_rows(0, 1)
+    conv_rows(7, 8)
     conv_out = pltpu.make_async_copy(conv, conv_hbm, local_sem.at[5])
     conv_out.start()
-    ring_end()
-    scan_send()
-    w_a_half()
-    scan_group()
+    pass_on_state()
     mine.wait()
-    scan_back()
+    w_b_half(0)
     w_b_full(1)
-    state_mine = share_state()
     w_b_full(2)
-    w_b_half(0)
     w_b_full(3)
     w_b_half(1)
     w_b_half(2)
     w_b_half(3)
-    for o in range(1, NZ):
-        remote(s_own, s_hbm.at[pl.ds(0, 16)], ag_send.at[o - 1], ag_recv.at[o - 1], tm, z).wait_recv()
+    state_end()
     w_end()
     for copy in everything + list(everything_rs.values()):
         copy.wait_send()
@@ -376,9 +423,10 @@
             jax.ShapeDtypeStruct((16 * NZ, 16, LANES), BF16),
             jax.ShapeDtypeStruct((32 * BLKP, DP), BF16),
         ),
-        in_specs=[any_space, any_space, any_space, pl.BlockSpec(memory_space=pltpu.VMEM)],
+        in_specs=[pl.BlockSpec(memory_space=pltpu.HBM)] * 4,
         out_specs=(any_space,) * 3,
         scratch_shapes=[
+            pltpu.VMEM((3, 3, D), F32),
             pltpu.VMEM((TOK, D), BF16),
             pltpu.VMEM((TOK + 2 * COLS, D), BF16),
             pltpu.VMEM((D, TOK), BF16),
@@ -396,12 +444,12 @@
             pltpu.VMEM((16, 16, LANES), BF16),
             pltpu.VMEM((NZ, BLK, D // NZ), BF16),
             pltpu.VMEM((BLKP, DP), BF16),
-            dma((6,)), dma((2,)), dma((2,)), dma((7,)), dma((7,)), dma((14,)), dma((14,)),
-            dma((7,)), dma((7,)), dma((3,)), dma((3,)), dma((7,)), dma((7,)), dma((7,)), dma((7,)),
+            dma((7,)), dma((2,)), dma((2,)), dma((7,)), dma((7,)), dma((7 * SUBS,)), dma((7 * SUBS,)),
+            dma((7,)), dma((7,)), dma((3,)), dma((3,)), dma((7,)), dma((7,)), dma((14,)), dma((14,)),
             dma((36,)), dma((36,)),
         ],
         compiler_params=pltpu.CompilerParams(
-            collective_id=0, has_side_effects=True, vmem_limit_bytes=48 << 20
+            collective_id=0, has_side_effects=True, vmem_limit_bytes=60 << 20
         ),
         name="state_and_gather",
     )(k, v, w, cw)
@@ -487,7 +535,7 @@
         project_kernel,
         grid=(DP // 256,),
         out_shape=jax.ShapeDtypeStruct((TOK, D), BF16),
-        in_specs=[any_space] * 4,
+        in_specs=[pl.BlockSpec(memory_space=pltpu.HBM)] + [any_space] * 3,
         out_specs=pl.BlockSpec((TOK, 256), lambda n: (0, n)),
         scratch_shapes=[
             pltpu.VMEM((TOK, D), BF16),

time: 93.8 us -> 83.8 us (0.89)
  Pallas kernels: 89.9 us -> 82.5 us
  local copies, waits for them, and re-layouts: 3.55 us -> 1.04 us
    pallas_call x1, Pallas kernels: 74.8 us -> 67.4 us  [gather(): pl.pallas_call(gather_kernel, out_shape=(jax.ShapeDtypeStruct((TOK, DP),...]
    unnamed x8 -> x4, local copies, waits for them, and re-layouts: 3.55 us -> 1.04 us
where the time goes in v2:
time: 83.8 us; the launch traced here: 83.7 us
  Pallas kernels  82.5 us (98%)
  local copies, waits for them, and re-layouts  1.04 us (1%)
    pallas_call x1, Pallas kernels, gather(): pl.pallas_call(gather_kernel, out_shape=(jax.ShapeDtypeStruct((TOK, DP),...  67.4 us
    pallas_call x1, Pallas kernels, project(): pl.pallas_call(project_kernel, grid=(DP // 256,), out_shape=jax.ShapeDtyp...  15.1 us

profile of v2, /device:TPU:1, one launch (start us, length us, event | category | flops | bytes accessed | tf_op | source)
XLA Modules:
  0.0 83.7 jit_solution(1807391806496626543)
XLA Ops:
  0.0 0.0 copy-start
  0.0 67.4 %state_and_gather.1 = (f32[640,2304]{1,0:T(8,128)}, bf16[128,16,128]{2,1,0:T(8,128)(2,1)}, bf16[2304,2304]{1,0:T(8,128)(2,1)}) custom-call(bf16[640,2240]{1,0:T(8,128)(2,1)} %bitcast.5, bf16[640,2240]{1,0:T(8,128)(2,1)} %bitcast.6, bf16[70,280]{1,0:T(8,128)(2,1)} %w_hbm.1, f32[3,3,2240]{2,1,0:T(4,128)} %cw_hbm.1), custom_call_target="tpu_custom_call" | custom-call | tf_op jit(solution)/shard_map/state_and_gather/pallas_call | solution.py:419
  67.4 0.0 copy-done
  67.4 0.0 copy-start.1
  67.4 1.0 %copy-done.1 = bf16[128,16,128]{2,1,0:T(8,128)(2,1)S(1)} copy-done((bf16[128,16,128]{2,1,0:T(8,128)(2,1)S(1)}, bf16[128,16,128]{2,1,0:T(8,128)(2,1)}, u32[]{:S(2)}) %copy-start.1) | copy-done | bytes 524312
  68.5 15.1 %attend_and_project.1 = bf16[640,2240]{1,0:T(8,128)(2,1)} custom-call(bf16[640,2240]{1,0:T(8,128)(2,1)S(1)} %bitcast.4, f32[640,2304]{1,0:T(8,128)} %get-tuple-element.8.conv_hbm, bf16[128,16,128]{2,1,0:T(8,128)(2,1)S(1)} %copy-done.1, bf16[2304,2304]{1,0:T(8,128)(2,1)} %get-tuple-element.10.w_hbm), custom_call_target="tpu_custom_call" | custom-call | tf_op jit(solution)/shard_map/attend_and_project/pallas_call | solution.py:534
Async XLA Ops:
  0.0 67.4 %copy-start = (bf16[1,8,80,2240]{3,2,1,0:T(8,128)(2,1)S(1)}, bf16[1,8,80,2240]{3,2,1,0:T(8,128)(2,1)}, u32[]{:S(2)}) copy-start(bf16[1,8,80,2240]{3,2,1,0:T(8,128)(2,1)} %param.5) | copy-start | bytes 8601604
  67.4 1.0 %copy-start.1 = (bf16[128,16,128]{2,1,0:T(8,128)(2,1)S(1)}, bf16[128,16,128]{2,1,0:T(8,128)(2,1)}, u32[]{:S(2)}) copy-start(bf16[128,16,128]{2,1,0:T(8,128)(2,1)} %get-tuple-element.9.s_hbm) | copy-start | bytes 1572868

commit v3 on v2

--- a/solution.py
+++ b/solution.py
@@ -19,6 +19,7 @@
 UNITS = 7
 NZ = 8
 EPS = 1e-06
+FIRST = 1280
 SUBS = 4
 PART = 16 // SUBS
 MESH = pl.DeviceIdType.MESH
@@ -54,8 +55,9 @@
 
 
 def gather_kernel(
-    k_hbm, v_hbm, w_hbm, cw_hbm, conv_hbm, s_hbm, wg_hbm,
+    q_hbm, k_hbm, v_hbm, w_hbm, cw_hbm, out_hbm, wg_hbm,
     cw_ref, kn, vn, kt, vp, cwp, conv, z_ref, fwd, bwd, own, scan, pre, xs, back, s_own, wa, wown,
+    s_all, sn, band, spreads, picks, qv, mix, wv, out_v,
     local_sem, halo_send, halo_recv, wa_send, wa_recv, rs_send, rs_recv, sc_send, sc_recv,
     xs_send, xs_recv, bk_send, bk_recv, ag_send, ag_recv, wg_send, wg_recv,
 ):
@@ -212,14 +214,14 @@
         for h in range(2):
             for o in (1, -1, 2, -2):
                 state_send(share_number[o] + h, s_own.at[pl.ds(8 * h, 8)], part_of(0, h), o)
-        copy = pltpu.make_async_copy(s_own, s_hbm.at[pl.ds(16 * z, 16)], local_sem.at[3])
+        copy = pltpu.make_async_copy(s_own, s_all.at[pl.ds(16 * z, 16)], local_sem.at[3])
         copy.start()
         return copy
 
     share_number = {1: 0, -1: 2, 2: 4, -2: 6}
 
     def part_of(o, h):
-        return s_hbm.at[pl.ds(16 * add_mod(z, o, NZ) + 8 * h, 8)]
+        return s_all.at[pl.ds(16 * add_mod(z, o, NZ) + 8 * h, 8)]
 
     def state_send(n, src, dst, o):
         start(remote(src, dst, ag_send.at[n], ag_recv.at[n], tm, add_mod(z, o, NZ)))
@@ -244,24 +246,28 @@
         for n, (o, h) in {8: (-3, 0), 9: (-3, 1), 10: (3, 0), 11: (3, 1), 12: (4, 0), 13: (4, 1)}.items():
             state_wait(n, part_of(o, h))
 
-    def rows_of(owner, half=None):
+    def rows_of(owner, half=None, p=0):
         lo, n = (0, BLKP) if half is None else ((0, 40) if half == 0 else (40, 32))
-        return wg_hbm.at[pl.ds(pl.multiple_of(BLKP * owner + lo, 8), n)]
-
-    def w_send(n, src, dst, to_tm):
-        start(remote(src, dst, wg_send.at[n], wg_recv.at[n], to_tm, z))
-
-    def w_wait(n, ref):
-        remote(ref, ref, wg_send.at[n], wg_recv.at[n], tm, z).wait_recv()
+        return wg_hbm.at[pl.ds(pl.multiple_of(BLKP * owner + lo, 8), n), columns(p)]
+
+    def columns(p):
+        return pl.ds(0, FIRST) if p == 0 else pl.ds(FIRST, DP - FIRST)
+
+    def w_send(n, src, dst, to_tm, p):
+        start(remote(src, dst, wg_send.at[36 * p + n], wg_recv.at[36 * p + n], to_tm, z))
+
+    def w_wait(n, ref, p):
+        remote(ref, ref, wg_send.at[36 * p + n], wg_recv.at[36 * p + n], tm, z).wait_recv()
 
     deltas = (0, -1, 1, 2)
 
-    def w_out_b(g, src=None):
+    def w_out_b(g, p):
         owner = along(deltas[g], 0)
-        ref = rows_of(owner) if src is None else src
-        w_send(4 + 4 * g, ref, rows_of(owner), along(0, 1))
-        w_send(5 + 4 * g, ref, rows_of(owner), along(0, -1))
-        w_send(20 + 4 * g, ref, rows_of(owner), partner)
+        ref = rows_of(owner, p=p) if g else wown.at[:, columns(p)]
+        to = rows_of(owner, p=p)
+        w_send(4 + 4 * g, ref, to, along(0, 1), p)
+        w_send(5 + 4 * g, ref, to, along(0, -1), p)
+        w_send(20 + 4 * g, ref, to, partner, p)
 
     def wa_wait(n):
         remote(w_hbm, wa.at[0], wa_send.at[n], wa_recv.at[n], tm, z).wait_recv()
@@ -288,47 +294,53 @@
                 col = lo + lax.broadcasted_iota(jnp.int32, (width, LANES), 1)
                 acc = acc + dot(wa[b], jnp.where(row == col, 1.0, 0.0).astype(BF16))
             wown[0:BLK, lo : lo + LANES] = acc.astype(BF16)
-        mine = pltpu.make_async_copy(wown, rows_of(tm), local_sem.at[4])
-        mine.start()
-        w_send(0, wown, rows_of(tm), along(1, 0))
-        w_send(1, wown, rows_of(tm), along(-1, 0))
+        mine = [
+            pltpu.make_async_copy(wown.at[:, columns(p)], rows_of(tm, p=p), local_sem.at[(4, 10)[p]])
+            for p in range(2)
+        ]
+        for copy in mine:
+            copy.start()
         return mine
 
-    def w_pass_full():
+    def w_out_a(p):
+        for n, k in enumerate((1, -1)):
+            w_send(n, wown.at[:, columns(p)], rows_of(tm, p=p), along(k, 0), p)
+
+    def w_pass_full(p):
         low, high = along(-1, 0), along(1, 0)
-        w_wait(0, rows_of(low))
-        w_wait(1, rows_of(high))
-        w_send(2, rows_of(low, 0), rows_of(low, 0), high)
-        w_send(3, rows_of(high, 1), rows_of(high, 1), low)
-
-    def w_wait_half():
-        w_wait(2, rows_of(along(2, 0), 0))
-        w_wait(3, rows_of(along(2, 0), 1))
-
-    def w_b_full(g):
+        w_wait(0, rows_of(low, p=p), p)
+        w_wait(1, rows_of(high, p=p), p)
+        w_send(2, rows_of(low, 0, p), rows_of(low, 0, p), high, p)
+        w_send(3, rows_of(high, 1, p), rows_of(high, 1, p), low, p)
+
+    def w_wait_half(p):
+        w_wait(2, rows_of(along(2, 0), 0, p), p)
+        w_wait(3, rows_of(along(2, 0), 1, p), p)
+
+    def w_b_full(g, p):
         low, high = along(deltas[g], -1), along(deltas[g], 1)
-        w_wait(4 + 4 * g, rows_of(low))
-        w_send(6 + 4 * g, rows_of(low, 0), rows_of(low, 0), along(0, 1))
-        w_wait(5 + 4 * g, rows_of(high))
-        w_send(7 + 4 * g, rows_of(high, 1), rows_of(high, 1), along(0, -1))
-        w_send(21 + 4 * g, rows_of(low), rows_of(low), partner)
-        w_send(22 + 4 * g, rows_of(high), rows_of(high), partner)
-
-    def w_b_half(g):
+        w_wait(4 + 4 * g, rows_of(low, p=p), p)
+        w_send(6 + 4 * g, rows_of(low, 0, p), rows_of(low, 0, p), along(0, 1), p)
+        w_wait(5 + 4 * g, rows_of(high, p=p), p)
+        w_send(7 + 4 * g, rows_of(high, 1, p), rows_of(high, 1, p), along(0, -1), p)
+        w_send(21 + 4 * g, rows_of(low, p=p), rows_of(low, p=p), partner, p)
+        w_send(22 + 4 * g, rows_of(high, p=p), rows_of(high, p=p), partner, p)
+
+    def w_b_half(g, p):
         far = along(deltas[g], 2)
-        w_wait(6 + 4 * g, rows_of(far, 0))
-        w_wait(7 + 4 * g, rows_of(far, 1))
-        w_send(23 + 4 * g, rows_of(far), rows_of(far), partner)
-
-    def w_end():
+        w_wait(6 + 4 * g, rows_of(far, 0, p), p)
+        w_wait(7 + 4 * g, rows_of(far, 1, p), p)
+        w_send(23 + 4 * g, rows_of(far, p=p), rows_of(far, p=p), partner, p)
+
+    def w_end(p):
         for n in range(20, 36):
-            w_wait(n, rows_of(0))
+            w_wait(n, rows_of(0, p=p), p)
 
     def conv_prepare():
         load_cw.wait()
         for j in range(TILES):
             _, lo, hi = spread_window(j)
-            spread = spread_matrix(j, lo, hi)
+            spread = spreads[j, : hi - lo, :]
             place = slice(LANES * j, LANES * (j + 1))
             vp[COLS : COLS + TOK, place] = dot(vn[COLS : COLS + TOK, lo:hi], spread).astype(BF16)
             for a in range(3):
@@ -347,7 +359,7 @@
             there = jnp.where(z == (0, NZ - 1)[n], 0.0, 1.0)
             for j in range(TILES):
                 _, lo, hi = spread_window(j)
-                rim = dot(vn[start_row : start_row + COLS, lo:hi], spread_matrix(j, lo, hi))
+                rim = dot(vn[start_row : start_row + COLS, lo:hi], spreads[j, : hi - lo, :])
                 vp[start_row : start_row + COLS, LANES * j : LANES * (j + 1)] = (rim * there).astype(BF16)
 
     def conv_rows(first, last):
@@ -366,65 +378,164 @@
                 right = jnp.where(row == COLS - 1, 0.0, pltpu.roll(sums[2], COLS - 1, 0))
                 conv[pl.ds(base, COLS), place] = sums[1] + left + right
 
+    def make_masks():
+        base = D - LANES * (TILES - 1)
+        pos = lax.broadcasted_iota(jnp.int32, (LANES, LANES), 1)
+        row = lax.broadcasted_iota(jnp.int32, (LANES, LANES), 0)
+        for j in range(TILES):
+            _, lo, _ = spread_window(j)
+            spreads[j] = spread_matrix(j, lo, lo + 2 * LANES)
+        n = 0
+        for j in range(TILES):
+            for h, from_lane, to_lane in head_lanes(j):
+                at = (pos >= from_lane) & (pos < to_lane) & (row == base + h)
+                picks[n] = jnp.where(at, 1.0, 0.0).astype(BF16)
+                n += 1
+
+    def clear_bands():
+        for j in range(TILES):
+            band[j] = jnp.zeros(band.shape[1:], BF16)
+
+    def make_bands():
+        for j in range(TILES):
+            for r in range(UNITS):
+                sn[16 * r : 16 * (r + 1), LANES * j : LANES * (j + 1)] = s_all[UNITS * j + r]
+        sums = sn[:, LANES * (TILES - 1) :]
+        lane = lax.broadcasted_iota(jnp.int32, (1, LANES), 1)
+        n = 0
+        for j in range(TILES):
+            _, _, lo, _ = heads_of(j)
+            _, w_lo, _ = spread_window(j)
+            state = dot(sn[:, w_lo : w_lo + 2 * LANES], spreads[j]).astype(BF16)
+            for h, from_lane, to_lane in head_lanes(j):
+                keep = jnp.where((lane >= from_lane) & (lane < to_lane), 1.0, 0.0).astype(BF16)
+                at = slice(HD * h - lo, HD * (h + 1) - lo)
+                band[j, at, :LANES] = state * keep
+                band[j, at, LANES:] = dot(sums, picks[n]).astype(BF16)
+                n += 1
+
+    def attend(tiles):
+        for j in tiles:
+            _, _, lo, hi = heads_of(j)
+            place = slice(LANES * j, LANES * (j + 1))
+            both = dot(jnp.maximum(qv[:, lo:hi], 0), band[j, : hi - lo, :])
+            mix[:, place] = (both[:, :LANES] / (both[:, LANES:] + EPS) + conv[:, place]).astype(BF16)
+
+    def project(lo, hi):
+        @pl.loop(lo, hi)
+        def _(n):
+            at = pl.ds(pl.multiple_of(256 * n, 256), 256)
+            out_v[:, at] = dot(mix[...], wv[:, at]).astype(BF16)
+
+    load_q = pltpu.make_async_copy(q_hbm, qv, local_sem.at[7])
+    load_w = [
+        pltpu.make_async_copy(wg_hbm.at[:, columns(p)], wv.at[:, columns(p)], local_sem.at[(8, 5)[p]])
+        for p in range(2)
+    ]
+    save_out = [
+        pltpu.make_async_copy(out_v.at[:, columns(p)], out_hbm.at[:, columns(p)], local_sem.at[(9, 11)[p]])
+        for p in range(2)
+    ]
+
     partial_state()
     ring_step(0)
+    load_q.start()
+    make_masks()
+    ring_step(1)
     wa_pass_on()
     conv_prepare()
-    ring_step(1)
+    clear_bands()
     ring_step(2)
     mine = w_assemble()
+    w_out_a(0)
+    w_out_b(0, 0)
+    w_out_a(1)
     ring_step(3)
     for copy in halo:
         start(copy)
-    w_out_b(0, wown)
     conv_rows(1, 4)
     ring_end()
     scan_send()
-    w_pass_full()
+    w_pass_full(0)
+    w_out_b(1, 0)
+    w_b_full(0, 0)
     conv_rows(4, 6)
     scan_group()
-    w_out_b(1)
-    w_b_full(0)
+    w_out_b(2, 0)
+    w_pass_full(1)
     conv_rows(6, 7)
     scan_back()
-    w_out_b(2)
+    w_wait_half(0)
+    w_out_b(3, 0)
+    w_out_b(0, 1)
     state_mine = share_state()
-    w_wait_half()
-    w_out_b(3)
+    w_b_full(1, 0)
+    w_b_half(0, 0)
+    w_out_b(1, 1)
     conv_rims()
     conv_rows(0, 1)
     conv_rows(7, 8)
-    conv_out = pltpu.make_async_copy(conv, conv_hbm, local_sem.at[5])
-    conv_out.start()
     pass_on_state()
-    mine.wait()
-    w_b_half(0)
-    w_b_full(1)
-    w_b_full(2)
-    w_b_full(3)
-    w_b_half(1)
-    w_b_half(2)
-    w_b_half(3)
+    w_b_full(2, 0)
+    w_b_full(3, 0)
+    w_b_full(0, 1)
+    w_out_b(2, 1)
+    w_wait_half(1)
+    w_out_b(3, 1)
     state_end()
-    w_end()
+    state_mine.wait()
+    w_b_half(1, 0)
+    w_b_half(2, 0)
+    w_b_full(1, 1)
+    make_bands()
+    w_b_half(3, 0)
+    w_b_full(2, 1)
+    load_q.wait()
+    attend(range(0, 5))
+    for copy in mine:
+        copy.wait()
+    w_end(0)
+    load_w[0].start()
+    w_b_full(3, 1)
+    attend(range(5, TILES))
+    w_b_half(0, 1)
+    w_b_half(1, 1)
+    load_w[0].wait()
+    project(0, 1)
+    w_b_half(2, 1)
+    w_b_half(3, 1)
+    project(1, 3)
+    w_end(1)
+    load_w[1].start()
+    project(3, 5)
+    save_out[0].start()
+    load_w[1].wait()
+    project(5, 9)
+    save_out[1].start()
     for copy in everything + list(everything_rs.values()):
         copy.wait_send()
-    state_mine.wait()
-    conv_out.wait()
-
-
-def gather(k, v, w, cw):
+    for copy in save_out:
+        copy.wait()
+
+
+def head_lanes(j):
+    heads = {}
+    for lane in range(LANES):
+        heads.setdefault(feature_of(LANES * j + lane) // HD, []).append(lane)
+    return [(h, min(lanes), max(lanes) + 1) for h, lanes in sorted(heads.items())]
+
+
+def gather(q, k, v, w, cw):
     dma = pltpu.SemaphoreType.DMA
     any_space = pl.BlockSpec(memory_space=pl.ANY)
     return pl.pallas_call(
         gather_kernel,
         out_shape=(
-            jax.ShapeDtypeStruct((TOK, DP), F32),
-            jax.ShapeDtypeStruct((16 * NZ, 16, LANES), BF16),
+            jax.ShapeDtypeStruct((TOK, DP), BF16),
             jax.ShapeDtypeStruct((32 * BLKP, DP), BF16),
         ),
-        in_specs=[pl.BlockSpec(memory_space=pltpu.HBM)] * 4,
-        out_specs=(any_space,) * 3,
+        in_specs=[pl.BlockSpec(memory_space=pltpu.HBM)] * 5,
+        out_specs=(any_space,) * 2,
         scratch_shapes=[
             pltpu.VMEM((3, 3, D), F32),
             pltpu.VMEM((TOK, D), BF16),
@@ -444,15 +555,24 @@
             pltpu.VMEM((16, 16, LANES), BF16),
             pltpu.VMEM((NZ, BLK, D // NZ), BF16),
             pltpu.VMEM((BLKP, DP), BF16),
-            dma((7,)), dma((2,)), dma((2,)), dma((7,)), dma((7,)), dma((7 * SUBS,)), dma((7 * SUBS,)),
+            pltpu.VMEM((16 * NZ, 16, LANES), BF16),
+            pltpu.VMEM((HD, DP), BF16),
+            pltpu.VMEM((TILES, 512, 256), BF16),
+            pltpu.VMEM((TILES, 256, LANES), BF16),
+            pltpu.VMEM((sum(len(head_lanes(j)) for j in range(TILES)), LANES, LANES), BF16),
+            pltpu.VMEM((TOK, D), BF16),
+            pltpu.VMEM((TOK, DP), BF16),
+            pltpu.VMEM((32 * BLKP, DP), BF16),
+            pltpu.VMEM((TOK, DP), BF16),
+            dma((12,)), dma((2,)), dma((2,)), dma((7,)), dma((7,)), dma((7 * SUBS,)), dma((7 * SUBS,)),
             dma((7,)), dma((7,)), dma((3,)), dma((3,)), dma((7,)), dma((7,)), dma((14,)), dma((14,)),
-            dma((36,)), dma((36,)),
+            dma((72,)), dma((72,)),
         ],
         compiler_params=pltpu.CompilerParams(
             collective_id=0, has_side_effects=True, vmem_limit_bytes=60 << 20
         ),
         name="state_and_gather",
-    )(k, v, w, cw)
+    )(q, k, v, w, cw)
 
 
 def heads_of(j):
@@ -465,97 +585,10 @@
     return first, last, lo, hi
 
 
-def project_kernel(q_hbm, conv_hbm, s_hbm, w_hbm, out_ref, qv, cv, sv, sn, band, mix, wv, sem):
-    n = pl.program_id(0)
-    steps = DP // 256
-    copies = [
-        pltpu.make_async_copy(s_hbm, sv, sem.at[0]),
-        pltpu.make_async_copy(q_hbm, qv, sem.at[1]),
-        pltpu.make_async_copy(conv_hbm, cv, sem.at[2]),
-    ]
-    weights = [
-        pltpu.make_async_copy(
-            w_hbm.at[:, pl.ds(256 * t, 256)], wv.at[:, pl.ds(256 * t, 256)], sem.at[3 + t]
-        )
-        for t in range(steps)
-    ]
-
-    @pl.when(n == 0)
-    def _():
-        for copy in copies + weights:
-            copy.start()
-        copies[0].wait()
-        for j in range(TILES):
-            for r in range(UNITS):
-                sn[16 * r : 16 * (r + 1), LANES * j : LANES * (j + 1)] = sv[UNITS * j + r]
-        sums = sn[:, LANES * (TILES - 1) :]
-        base = D - LANES * (TILES - 1)
-        for j in range(TILES):
-            first, last, lo, hi = heads_of(j)
-            band[j] = jnp.zeros(band.shape[1:], BF16)
-            _, w_lo, _ = spread_window(j)
-            w_hi = w_lo + 2 * LANES
-            spread = spread_matrix(j, w_lo, w_hi)
-            state = dot(sn[:, w_lo:w_hi], spread).astype(BF16)
-            pos = LANES * j + lax.broadcasted_iota(jnp.int32, (LANES, LANES), 1)
-            block = lax.shift_right_logical(pos * 14564, 20)
-            inside = pos - BLKP * block
-            feature = BLK * block + inside
-            row = lax.broadcasted_iota(jnp.int32, (LANES, LANES), 0)
-            for h in range(first, last + 1):
-                member = (inside < BLK) & (feature >= HD * h) & (feature < HD * (h + 1))
-                pick = jnp.where(member & (row == base + h), 1.0, 0.0).astype(BF16)
-                keep = jnp.where(member[:1], 1.0, 0.0).astype(BF16)
-                at = slice(HD * h - lo, HD * (h + 1) - lo)
-                band[j, at, :LANES] = state * keep
-                band[j, at, LANES:] = dot(sums, pick).astype(BF16)
-        copies[1].wait()
-        qv[...] = jnp.maximum(qv[...], 0)
-        copies[2].wait()
-        for j in range(TILES):
-            _, _, lo, hi = heads_of(j)
-            place = slice(LANES * j, LANES * (j + 1))
-            both = dot(qv[:, lo:hi], band[j, : hi - lo, :])
-            attn = both[:, :LANES] / (both[:, LANES:] + EPS)
-            mix[:, place] = (attn + cv[:, place]).astype(BF16)
-
-    for t in range(steps):
-
-        @pl.when(n == t)
-        def _():
-            weights[t].wait()
-
-    at = pl.ds(pl.multiple_of(256 * n, 256), 256)
-    out_ref[...] = dot(mix[...], wv[:, at]).astype(BF16)
-
-
-def project(q, conv, s, w):
-    any_space = pl.BlockSpec(memory_space=pl.ANY)
-    return pl.pallas_call(
-        project_kernel,
-        grid=(DP // 256,),
-        out_shape=jax.ShapeDtypeStruct((TOK, D), BF16),
-        in_specs=[pl.BlockSpec(memory_space=pltpu.HBM)] + [any_space] * 3,
-        out_specs=pl.BlockSpec((TOK, 256), lambda n: (0, n)),
-        scratch_shapes=[
-            pltpu.VMEM((TOK, D), BF16),
-            pltpu.VMEM((TOK, DP), F32),
-            pltpu.VMEM((16 * NZ, 16, LANES), BF16),
-            pltpu.VMEM((HD, DP), BF16),
-            pltpu.VMEM((TILES, 512, 256), BF16),
-            pltpu.VMEM((TOK, DP), BF16),
-            pltpu.VMEM((32 * BLKP, DP), BF16),
-            pltpu.SemaphoreType.DMA((3 + DP // 256,)),
-        ],
-        compiler_params=pltpu.CompilerParams(vmem_limit_bytes=48 << 20),
-        name="attend_and_project",
-    )(q, conv, s, w)
-
-
 def shards(queries, keys, values, conv_weight, w_out):
     q, k, v = (a.reshape(TOK, D) for a in (queries, keys, values))
-    conv, states, weights = gather(k, v, w_out, conv_weight)
-    return project(q, conv, states, weights).reshape(1, ROWS, COLS, D)
+    out, _ = gather(q, k, v, w_out, conv_weight)
+    return out[:, :D].reshape(1, ROWS, COLS, D)
 
 
 def solution(mesh):

time: 83.8 us -> 79.6 us (0.950)
  Pallas kernels: 82.5 us -> 75.8 us
  local copies, waits for them, and re-layouts: 1.04 us -> 3.62 us
    pallas_call x1 -> x0, Pallas kernels: 15.1 us -> none  [project(): pl.pallas_call(project_kernel, grid=(DP // 256,), out_shape=jax.ShapeDtyp...]
    pallas_call x1, Pallas kernels: 67.4 us -> 75.8 us  [gather(): pl.pallas_call(gather_kernel, out_shape=(jax.ShapeDtypeStruct((TOK, DP),...]
    unnamed x4 -> x1, local copies, waits for them, and re-layouts: 1.04 us -> 3.62 us
where the time goes in v3:
time: 79.6 us; the launch traced here: 79.5 us
  Pallas kernels  75.8 us (95%)
  local copies, waits for them, and re-layouts  3.62 us (5%)
    pallas_call x1, Pallas kernels, gather(): pl.pallas_call(gather_kernel, out_shape=(jax.ShapeDtypeStruct((TOK, DP),...  75.8 us
    unnamed x1, local copies, waits for them, and re-layouts  3.62 us

profile of v3, /device:TPU:1, one launch (start us, length us, event | category | flops | bytes accessed | tf_op | source)
XLA Modules:
  0.0 79.5 jit_solution(4480811094625691599)
XLA Ops:
  0.0 75.8 %state_and_gather.1 = (bf16[640,2304]{1,0:T(8,128)(2,1)}, bf16[2304,2304]{1,0:T(8,128)(2,1)}) custom-call(bf16[640,2240]{1,0:T(8,128)(2,1)} %bitcast.5, bf16[640,2240]{1,0:T(8,128)(2,1)} %bitcast.6, bf16[640,2240]{1,0:T(8,128)(2,1)} %bitcast.7, bf16[70,280]{1,0:T(8,128)(2,1)} %w_hbm.1, f32[3,3,2240]{2,1,0:T(4,128)} %cw_hbm.1), custom_call_target="tpu_custom_call" | custom-call | tf_op jit(solution)/shard_map/state_and_gather/pallas_call | solution.py:531
  75.8 3.6 %copy.7 = bf16[1,8,80,2240]{3,2,1,0:T(8,128)(2,1)} copy(bf16[1,8,80,2240]{3,2,1,0:T(8,128)(2,1)} %bitcast.8) | data formatting | bytes 5734400

commit v4 on v3

--- a/solution.py
+++ b/solution.py
@@ -19,7 +19,7 @@
 UNITS = 7
 NZ = 8
 EPS = 1e-06
-FIRST = 1280
+FIRST = 1536
 SUBS = 4
 PART = 16 // SUBS
 MESH = pl.DeviceIdType.MESH
@@ -444,7 +444,6 @@
     ring_step(1)
     wa_pass_on()
     conv_prepare()
-    clear_bands()
     ring_step(2)
     mine = w_assemble()
     w_out_a(0)
@@ -459,6 +458,7 @@
     w_pass_full(0)
     w_out_b(1, 0)
     w_b_full(0, 0)
+    clear_bands()
     conv_rows(4, 6)
     scan_group()
     w_out_b(2, 0)
@@ -507,10 +507,10 @@
     project(1, 3)
     w_end(1)
     load_w[1].start()
-    project(3, 5)
+    project(3, 6)
     save_out[0].start()
     load_w[1].wait()
-    project(5, 9)
+    project(6, 9)
     save_out[1].start()
     for copy in everything + list(everything_rs.values()):
         copy.wait_send()

time: 79.6 us -> 80.4 us (1.010)
  no operation moved by 1% of the time
where the time goes in v4:
time: 80.4 us; the launch traced here: 80.2 us
  Pallas kernels  76.6 us (95%)
  local copies, waits for them, and re-layouts  3.62 us (5%)
    pallas_call x1, Pallas kernels, gather(): pl.pallas_call(gather_kernel, out_shape=(jax.ShapeDtypeStruct((TOK, DP),...  76.6 us
    unnamed x1, local copies, waits for them, and re-layouts  3.62 us

profile of v4, /device:TPU:1, one launch (start us, length us, event | category | flops | bytes accessed | tf_op | source)
XLA Modules:
  0.0 80.2 jit_solution(8404765340204910074)
XLA Ops:
  0.0 76.6 %state_and_gather.1 = (bf16[640,2304]{1,0:T(8,128)(2,1)}, bf16[2304,2304]{1,0:T(8,128)(2,1)}) custom-call(bf16[640,2240]{1,0:T(8,128)(2,1)} %bitcast.5, bf16[640,2240]{1,0:T(8,128)(2,1)} %bitcast.6, bf16[640,2240]{1,0:T(8,128)(2,1)} %bitcast.7, bf16[70,280]{1,0:T(8,128)(2,1)} %w_hbm.1, f32[3,3,2240]{2,1,0:T(4,128)} %cw_hbm.1), custom_call_target="tpu_custom_call" | custom-call | tf_op jit(solution)/shard_map/state_and_gather/pallas_call | solution.py:531
  76.6 3.6 %copy.7 = bf16[1,8,80,2240]{3,2,1,0:T(8,128)(2,1)} copy(bf16[1,8,80,2240]{3,2,1,0:T(8,128)(2,1)} %bitcast.8) | data formatting | bytes 5734400
